TPU v7x, 32 devices: a whole 2x2x4 slice. The times are simulated.
32 devices in a mesh: segment: 4 (over z), expert: 4 (over y, core), token: 2 (over x).
Axes of the slice: x: 2, y: 2, z: 4, core: 2. Of those that a mesh axis runs over, the one named last changes fastest.
Arguments:
- fwd_acts: bfloat16 [4, 256, 2048], P('segment', 'expert'), may hold values from -6 to 6
- fwd_ids: int32 [4, 256, 6], P('segment', 'expert'), may hold values from 0 to 7, as said below
- fwd_slots: int32 [4, 256, 6], P('segment', 'expert'), may hold values from 0 to 36, as said below
- bwd_acts: bfloat16 [4, 256, 2048], P('segment', 'expert'), may hold values from -6 to 6
- bwd_ids: int32 [4, 256, 6], P('segment', 'expert'), may hold values from 0 to 7, as said below
- bwd_slots: int32 [4, 256, 6], P('segment', 'expert'), may hold values from 0 to 36, as said below
- bwd_grad: bfloat16 [4, 256, 2048], P('segment', 'expert'), may hold values from -6 to 6
- norm_gain: float32 [4, 2048], P('segment'), may hold values from 0.25 to 1.75
- router: float32 [4, 2048, 8], P('segment'), may hold values from -0.125 to 0.125
- w_gate: bfloat16 [8, 2048, 1408], P('expert', None, 'token'), may hold values from -0.125 to 0.125
- w_up: bfloat16 [8, 2048, 1408], P('expert', None, 'token'), may hold values from -0.125 to 0.125
- w_down: bfloat16 [8, 1408, 2048], P('expert', 'token'), may hold values from -0.15625 to 0.15625
Outputs:
- next_acts: bfloat16 [4, 256, 2048], P('segment', 'expert', 'token')
- prev_grads: bfloat16 [4, 256, 2048], P('segment', 'expert', 'token')
Inputs may be any that keep to these rules, and one draw needn't show every extreme that they name: `fwd_ids`: each row names 6 different experts. `fwd_slots`: entry (t, k) counts the assignments to expert fwd_ids[t, k] that come before it in t's block of 64 rows (rows in order, a row's 6 choices in order), capped at 36; 36 marks a dropped assignment. In every block one expert, the same for all blocks of a section, is named by more than 36 rows. `bwd_ids`: each row names 6 different experts. `bwd_slots`: entry (t, k) counts the assignments to expert bwd_ids[t, k] that come before it in t's block of 64 rows (rows in order, a row's 6 choices in order), capped at 36; 36 marks a dropped assignment. In every block one expert, the same for all blocks of a section, is named by more than 36 rows.
All inputs are finite; a program needn't handle non-finite values.
Results may differ from a plain program's by a relative error of at most 0.009.
Values may be sent and summed in bfloat16 or wider, within the bound.
A program may use at most 128 MiB of HBM per device.

v0:
```python
import jax
import jax.numpy as jnp
from jax import lax
from jax.sharding import PartitionSpec as P

route_scale = 2.446
norm_eps = 1e-06
highest = lax.Precision.HIGHEST


def extended(block, sides, width):
    for axis, dim in sides:
        count = lax.axis_size(axis)
        forward = [(i, i + 1) for i in range(count - 1)]
        backward = [(target, source) for source, target in forward]
        low = lax.ppermute(
            lax.slice_in_dim(block, block.shape[dim] - width, None, axis=dim), axis, forward
        )
        high = lax.ppermute(lax.slice_in_dim(block, 0, width, axis=dim), axis, backward)
        block = jnp.concatenate([low, block, high], axis=dim)
    return block


def normalize(values, norm_scale):
    widened = values.astype(jnp.float32)
    inverse = lax.rsqrt(jnp.mean(widened * widened, axis=-1, keepdims=True) + norm_eps)
    scaled = widened * inverse
    return ((scaled * norm_scale).astype(jnp.bfloat16), scaled, inverse)


def gating(normed, expert_ids, router):
    logits = jnp.dot(normed.astype(jnp.float32), router, precision=highest)
    sigmoids = jax.nn.sigmoid(logits)
    picked = (expert_ids[..., None] == jnp.arange(router.shape[1], dtype=jnp.int32)).astype(
        jnp.float32
    )
    chosen = jnp.sum(picked * sigmoids[..., None, :], axis=-1)
    totals = jnp.sum(chosen, axis=-1, keepdims=True)
    return (route_scale * chosen / totals, chosen, totals, picked)


def slot_map(expert_ids, slot_ids, slot_count, capacity):
    target = expert_ids * capacity + slot_ids
    matches = (target[..., None] == jnp.arange(slot_count, dtype=jnp.int32)) & (
        slot_ids < capacity
    )[..., None]
    return matches.astype(jnp.float32)


def pack_rows(mapping, token_rows):
    chosen = jnp.sum(mapping, axis=-2).astype(jnp.bfloat16)
    packed = jnp.einsum("tc,td->cd", chosen, token_rows, preferred_element_type=jnp.float32)
    return packed.astype(jnp.bfloat16)


def activate(rows, gate_w, up_w):
    gate_vals = jnp.einsum("secd,edf->secf", rows, gate_w, preferred_element_type=jnp.float32)
    up_vals = jnp.einsum("secd,edf->secf", rows, up_w, preferred_element_type=jnp.float32)
    return (gate_vals * jax.nn.sigmoid(gate_vals) * up_vals).astype(jnp.bfloat16)


def backward_local(saved_rows, cotangent_rows, gate_w, up_w, down_w):
    gate_vals = jnp.einsum("secd,edf->secf", saved_rows, gate_w, preferred_element_type=jnp.float32)
    up_vals = jnp.einsum("secd,edf->secf", saved_rows, up_w, preferred_element_type=jnp.float32)
    sigma = jax.nn.sigmoid(gate_vals)
    active_bwd = (gate_vals * sigma * up_vals).astype(jnp.bfloat16)
    grad_act = jnp.einsum(
        "secd,efd->secf", cotangent_rows, down_w, preferred_element_type=jnp.float32
    )
    grad_gate = (grad_act * up_vals * sigma * (1.0 + gate_vals * (1.0 - sigma))).astype(
        jnp.bfloat16
    )
    grad_up = (grad_act * gate_vals * sigma).astype(jnp.bfloat16)
    return (active_bwd, grad_gate, grad_up)


def down_part(active, down_w, count, width_part):
    columns = down_w
    columns = columns.reshape(down_w.shape[0], down_w.shape[1], count, width_part)
    return jnp.einsum("secf,efnq->nsecq", active, columns, preferred_element_type=jnp.float32)


def into_part(grads, weight, count, width_part):
    rows_of = weight
    rows_of = rows_of.reshape(weight.shape[0], count, width_part, weight.shape[2])
    return jnp.einsum("secf,enqf->nsecq", grads, rows_of, preferred_element_type=jnp.float32)


def finish_back(
    normed_b,
    scaled_b,
    inverse_b,
    ids_b,
    cotangent_own,
    mixed_back,
    grad_gates,
    mean_sum,
    norm_scale,
    router,
    offset_cols,
    width_part,
):
    gates_b, chosen, totals, picked = gating(normed_b, ids_b, router)
    grad_probs = route_scale * grad_gates / totals - route_scale * jnp.sum(
        grad_gates * chosen, axis=-1, keepdims=True
    ) / (totals * totals)
    grad_logit = grad_probs * chosen * (1.0 - chosen)
    dense_grad = jnp.sum(picked * grad_logit[..., None], axis=-2)
    router_term = jnp.dot(dense_grad, router.T, precision=highest)
    model_width = scaled_b.shape[1]
    mean_all = (
        mean_sum + jnp.sum(router_term * norm_scale * scaled_b, axis=-1, keepdims=True)
    ) / model_width
    gain_own = lax.dynamic_slice_in_dim(norm_scale, offset_cols, width_part, 0)
    scaled_own = lax.dynamic_slice_in_dim(scaled_b, offset_cols, width_part, 1)
    router_own = lax.dynamic_slice_in_dim(router_term, offset_cols, width_part, 1)
    grad_scaled = (mixed_back + router_own) * gain_own
    grad_in = inverse_b * (grad_scaled - scaled_own * mean_all)
    return (cotangent_own.astype(jnp.float32) + grad_in).astype(jnp.bfloat16)


def body(
    fwd_acts,
    fwd_ids,
    fwd_slots,
    bwd_acts,
    bwd_ids,
    bwd_slots,
    bwd_grad,
    norm_gain,
    router,
    w_gate,
    w_up,
    w_down,
):
    norm_scale = norm_gain[0]
    segment_router = router[0]
    experts_all = segment_router.shape[1]
    per_device = w_gate.shape[0]
    senders = lax.axis_size("expert")
    hidden_parts = lax.axis_size("token")
    block_tokens = fwd_acts.shape[1]
    model_width = fwd_acts.shape[2]
    choices_per = fwd_ids.shape[2]
    capacity = max(2, min(3 * block_tokens * choices_per // (4 * experts_all), block_tokens - 1))
    slot_count = experts_all * capacity
    width_part = model_width // hidden_parts
    offset_cols = lax.axis_index("token") * width_part

    def own_cols(token_rows):
        return lax.dynamic_slice_in_dim(token_rows, offset_cols, width_part, 1)

    normed_a, _, _ = normalize(fwd_acts[0], norm_scale)
    normed_b, scaled_b, inverse_b = normalize(bwd_acts[0], norm_scale)
    cotangent = bwd_grad[0]
    map_a = slot_map(fwd_ids[0], fwd_slots[0], slot_count, capacity)
    map_b = slot_map(bwd_ids[0], bwd_slots[0], slot_count, capacity)
    buffer_shape = (senders, per_device, capacity, width_part)
    sent_a = pack_rows(map_a, own_cols(normed_a)).reshape(buffer_shape)
    sent_b = pack_rows(map_b, own_cols(normed_b)).reshape(buffer_shape)
    sent_c = pack_rows(map_b, own_cols(cotangent)).reshape(buffer_shape)
    gates_a = gating(normed_a, fwd_ids[0], segment_router)[0]
    gates_b = gating(normed_b, bwd_ids[0], segment_router)[0]
    fwd_own = own_cols(fwd_acts[0]).astype(jnp.float32)
    spread = lax.all_gather(
        lax.all_to_all(sent_a, "expert", split_axis=0, concat_axis=0, tiled=True),
        "token",
        axis=3,
        tiled=True,
    )
    active_a = activate(spread, w_gate, w_up)
    summed = lax.psum_scatter(
        down_part(active_a, w_down, 1 * lax.axis_size("token"), width_part).astype(jnp.bfloat16),
        "token",
        scatter_dimension=0,
        tiled=True,
    ).astype(jnp.float32)
    got_fwd = lax.all_to_all(
        summed[0].astype(jnp.bfloat16), "expert", split_axis=0, concat_axis=0, tiled=True
    ).astype(jnp.float32)
    got_fwd = got_fwd.reshape(slot_count, width_part)
    mixed_fwd = jnp.einsum("tkc,cd->td", map_a * gates_a[..., None], got_fwd, precision=highest)
    next_rows = (fwd_own + mixed_fwd).astype(jnp.bfloat16)
    spread = (
        lax.all_gather(
            lax.all_to_all(sent_b, "expert", split_axis=0, concat_axis=0, tiled=True),
            "token",
            axis=3,
            tiled=True,
        ),
        lax.all_gather(
            lax.all_to_all(sent_c, "expert", split_axis=0, concat_axis=0, tiled=True),
            "token",
            axis=3,
            tiled=True,
        ),
    )
    active_b, grad_gate, grad_up = backward_local(spread[0], spread[1], w_gate, w_up, w_down)
    out_b = down_part(active_b, w_down, 1 * lax.axis_size("token"), width_part)
    back_in = into_part(grad_gate, w_gate, 1 * lax.axis_size("token"), width_part) + into_part(
        grad_up, w_up, 1 * lax.axis_size("token"), width_part
    )
    summed = lax.psum_scatter(
        jnp.stack((out_b, back_in), axis=1).astype(jnp.bfloat16),
        "token",
        scatter_dimension=0,
        tiled=True,
    ).astype(jnp.float32)
    returned = lax.all_to_all(
        summed[0].astype(jnp.bfloat16), "expert", split_axis=1, concat_axis=1, tiled=True
    ).astype(jnp.float32)
    returned = returned.reshape(2, slot_count, width_part)
    got_bwd = returned[0]
    got_back = returned[1]
    cotangent_own = own_cols(cotangent)
    mixed_back = jnp.einsum("tkc,cd->td", map_b * gates_b[..., None], got_back, precision=highest)
    paired = jnp.einsum("td,cd->tc", cotangent_own.astype(jnp.float32), got_bwd, precision=highest)
    grad_part = jnp.einsum("tkc,tc->tk", map_b, paired, precision=highest)
    gain_own = lax.dynamic_slice_in_dim(norm_scale, offset_cols, width_part, 0)
    mean_part = jnp.sum(mixed_back * gain_own * own_cols(scaled_b), axis=-1, keepdims=True)
    grad_gates, mean_sum = lax.psum((grad_part, mean_part), "token")
    prev_rows = finish_back(
        normed_b,
        scaled_b,
        inverse_b,
        bwd_ids[0],
        cotangent_own,
        mixed_back,
        grad_gates,
        mean_sum,
        norm_scale,
        segment_router,
        offset_cols,
        width_part,
    )
    edges = extended(jnp.stack((prev_rows, next_rows)), (("segment", 0),), 1)
    return (edges[0][None], edges[3][None])


def solution(mesh):
    return jax.shard_map(
        body,
        mesh=mesh,
        in_specs=(
            P("segment", "expert", None),
            P("segment", "expert", None),
            P("segment", "expert", None),
            P("segment", "expert", None),
            P("segment", "expert", None),
            P("segment", "expert", None),
            P("segment", "expert", None),
            P("segment", None),
            P("segment", None, None),
            P("expert", None, "token"),
            P("expert", None, "token"),
            P("expert", "token", None),
        ),
        out_specs=(P("segment", "expert", "token"), P("segment", "expert", "token")),
        check_vma=False,
    )
```

profile of v0, /device:TPU:0, one launch (start us, length us, event | category | flops | bytes accessed | tf_op | source)
XLA Modules:
  0.0 283.8 jit_solution(3728924588242830624)
XLA Ops:
  7.2 0.7 copy.149
  7.9 0.7 bitcast_add_fusion
  8.6 0.7 bitcast_compare_fusion
  9.3 1.1 fusion.75
  10.4 1.1 fusion.69
  11.5 1.4 fusion.63
  12.9 0.7 dynamic-slice.7
  13.6 0.9 convert_reduce_fusion
  14.5 0.3 convolution_convert_fusion.1
  15.0 1.4 copy.78
  16.4 4.3 %all-to-all-start.2 = ((bf16[4,2,36,1024]{3,1,2,0:T(2,128)(2,1)}), bf16[4,2,36,1024]{3,1,2,0:T(2,128)(2,1)S(1)}, u32[]{:S(2)}, u32[]{:S(2)}) async-start(bf16[4,2,36,1024]{3,1,2,0:T(2,128)(2,1)} %copy.78), calls=%async_computation.2 | async-start | bytes 1179648 | tf_op jit(solution)/shard_map/all_to_all | solution.py:186
  20.7 0.3 convolution_convert_fusion
  21.2 1.4 copy.81
  22.8 7.4 %all-to-all-done.2 = bf16[4,2,36,1024]{3,1,2,0:T(2,128)(2,1)S(1)} async-done(((bf16[4,2,36,1024]{3,1,2,0:T(2,128)(2,1)}), bf16[4,2,36,1024]{3,1,2,0:T(2,128)(2,1)S(1)}, u32[]{:S(2)}, u32[]{:S(2)}) %all-to-all-start.2) | async-done | bytes 589856 | tf_op jit(solution)/shard_map/all_to_all | solution.py:186
  30.2 3.5 %all-to-all-start.3 = ((bf16[4,2,36,1024]{3,1,2,0:T(2,128)(2,1)}), bf16[4,2,36,1024]{3,1,2,0:T(2,128)(2,1)S(1)}, u32[]{:S(2)}, u32[]{:S(2)}) async-start(bf16[4,2,36,1024]{3,1,2,0:T(2,128)(2,1)} %copy.81), calls=%async_computation.3 | async-start | bytes 1179648 | tf_op jit(solution)/shard_map/all_to_all | solution.py:192
  33.8 1.0 copy.79
  34.9 0.4 fusion.66
  35.3 7.8 %all-to-all-done.3 = bf16[4,2,36,1024]{3,1,2,0:T(2,128)(2,1)S(1)} async-done(((bf16[4,2,36,1024]{3,1,2,0:T(2,128)(2,1)}), bf16[4,2,36,1024]{3,1,2,0:T(2,128)(2,1)S(1)}, u32[]{:S(2)}, u32[]{:S(2)}) %all-to-all-start.3) | async-done | bytes 589856 | tf_op jit(solution)/shard_map/all_to_all | solution.py:192
  43.2 1.0 copy.82
  44.2 0.9 convert_reduce_fusion.1
  45.1 0.4 convolution_convert_fusion.2
  45.6 1.4 copy.72
  47.1 3.5 %all-to-all-start = ((bf16[4,2,36,1024]{3,1,2,0:T(2,128)(2,1)}), bf16[4,2,36,1024]{3,1,2,0:T(2,128)(2,1)S(1)}, u32[]{:S(2)}, u32[]{:S(2)}) async-start(bf16[4,2,36,1024]{3,1,2,0:T(2,128)(2,1)} %copy.72), calls=%async_computation | async-start | bytes 1179648 | tf_op jit(solution)/shard_map/all_to_all | solution.py:166
  50.6 10.5 %reshape.176 = bf16[2,2,1024,704]{2,1,3,0:T(2,128)(2,1)} reshape(bf16[2,2048,704]{1,2,0:T(8,128)(2,1)} %param.22) | data formatting | bytes 11534336 | tf_op jit(solution)/shard_map/reshape | solution.py:85
  61.1 10.5 %reshape.175 = bf16[2,2,1024,704]{2,1,3,0:T(2,128)(2,1)} reshape(bf16[2,2048,704]{1,2,0:T(8,128)(2,1)} %param.21) | data formatting | bytes 11534336 | tf_op jit(solution)/shard_map/reshape | solution.py:85
  71.6 10.5 %reshape.171 = bf16[2,704,2,1024]{3,2,1,0:T(2,128)(2,1)} reshape(bf16[2,704,2048]{2,1,0:T(8,128)(2,1)} %param.23) | data formatting | bytes 11534336 | tf_op jit(solution)/shard_map/reshape | solution.py:79
  82.0 1.0 copy.73
  83.1 0.2 all-reduce.6.cloned.1.call-start
  83.3 4.9 %fusion.38 = f32[4,2,36,704]{3,2,0,1:T(8,128)S(1)} fusion(bf16[4,2,36,2048]{3,2,0,1:T(8,128)(2,1)} %all-gather.6.cloned.1.call-done, bf16[2,2048,704]{1,2,0:T(8,128)(2,1)} %param.21), kind=kOutput, calls=%fused_computation.26 | convolution fusion | flops 830472192 | bytes 7757824 | tf_op jit(solution)/shard_map/secd,edf->secf/dot_general | solution.py:63
  88.5 5.1 %fusion.50 = f32[4,2,36,704]{3,2,0,1:T(8,128)S(1)} fusion(bf16[4,2,36,2048]{3,2,0,1:T(8,128)(2,1)} %all-gather.8.cloned.1.call-done, bf16[2,704,2048]{2,1,0:T(8,128)(2,1)} %param.23), kind=kOutput, calls=%fused_computation.30 | convolution fusion | flops 830472192 | bytes 7757824 | tf_op jit(solution)/shard_map/secd,efd->secf/dot_general | solution.py:67
  93.6 5.3 %fusion.2 = f32[2,4,36,2,1024]{4,2,3,1,0:T(8,128)S(1)} fusion(bf16[2,2,1024,704,1]{2,1,3,0,4:T(2,128)(2,1)} %bitcast.191, f32[4,2,36,704]{3,2,0,1:T(8,128)S(1)} %fusion.50, f32[4,2,36,704]{3,2,0,1:T(8,128)S(1)} %fusion.38), kind=kOutput, calls=%fused_computation.2 | convolution fusion | flops 831688704 | bytes 9748480 | tf_op jit(solution)/shard_map/secf,enqf->nsecq/dot_general | solution.py:86
  98.9 1.9 fusion.47
  100.8 2.4 fusion.29
  103.3 2.5 fusion.26
  105.8 0.3 pad_maximum_fusion
  106.1 3.5 %copy.85 = bf16[2,2,4,2,36,1024]{5,2,4,3,1,0:T(4,128)(2,1)} copy(bf16[2,2,4,2,36,1024]{5,4,0,2,3,1:T(8,128)(2,1)S(1)} %pad_maximum_fusion) | data formatting | bytes 4718592 | tf_op jit(solution)/shard_map/stack | solution.py:204
  109.6 4.7 %all-gather.4.cloned.1.call-done = bf16[4,2,36,2048]{3,2,0,1:T(8,128)(2,1)} async-done(((bf16[4,2,36,1024]{3,2,0,1:T(8,128)(2,1)}), bf16[4,2,36,2048]{3,2,0,1:T(8,128)(2,1)}) %all-gather.4.cloned.1.call-update) | async-done | bytes 1179664 | tf_op jit(solution)/shard_map/all_gather | solution.py:165
  114.3 5.1 %fusion.35 = f32[4,2,36,704]{3,2,0,1:T(8,128)S(1)} fusion(bf16[4,2,36,2048]{3,2,0,1:T(8,128)(2,1)} %all-gather.4.cloned.1.call-done, bf16[2,2048,704]{1,2,0:T(8,128)(2,1)} %param.21), kind=kOutput, calls=%fused_computation.25 | convolution fusion | flops 830472192 | bytes 7757824 | tf_op jit(solution)/shard_map/secd,edf->secf/dot_general | solution.py:57
  119.4 4.7 %fusion.56 = bf16[4,2,36,704,1]{3,2,4,0,1:T(8,128)(2,1)S(1)} fusion(bf16[4,2,36,2048]{3,2,0,1:T(8,128)(2,1)S(1)} %copy-done.4, bf16[2,2048,704]{1,2,0:T(8,128)(2,1)} %param.22, f32[4,2,36,704]{3,2,0,1:T(8,128)S(1)} %fusion.35), kind=kOutput, calls=%fused_computation.35 | convolution fusion | flops 831688704 | bytes 8163328 | tf_op jit(solution)/shard_map/secd,edf->secf/dot_general | solution.py:58
  124.1 2.3 fusion.32
  126.4 1.9 copy.75
  128.3 0.6 dynamic-slice.3
  128.9 93.9 %all-reduce.6.cloned.1.call-done = (bf16[2,4,2,36,1024]{4,1,3,2,0:T(4,128)(2,1)}, bf16[2,2,4,2,36,1024]{5,2,4,3,1,0:T(4,128)(2,1)}) async-done(((bf16[2,4,2,36,1024]{4,1,3,2,0:T(4,128)(2,1)}, bf16[2,2,4,2,36,1024]{5,2,4,3,1,0:T(4,128)(2,1)}), (bf16[2,4,2,36,1024]{4,1,3,2,0:T(4,128)(2,1)}, bf16[2,2,4,2,36,1024]{5,2,4,3,1,0:T(4,128)(2,1)})) %all-reduce.6.cloned.1.call-update) | async-done | bytes 3538960
  222.9 1.9 dynamic-slice_bitcast_fusion.1
  224.8 1.4 copy.76
  226.2 3.5 %all-to-all-start.1 = ((bf16[4,2,36,1024]{3,1,2,0:T(2,128)(2,1)}), bf16[4,2,36,1024]{3,1,2,0:T(2,128)(2,1)S(1)}, u32[]{:S(2)}, u32[]{:S(2)}) async-start(bf16[4,2,36,1024]{3,1,2,0:T(2,128)(2,1)} %copy.76), calls=%async_computation.1 | async-start | bytes 1179648 | tf_op jit(solution)/shard_map/all_to_all | solution.py:178
  229.7 2.3 dynamic-slice_bitcast_fusion
  232.1 2.3 copy.86
  234.3 4.9 %all-to-all-done.1 = bf16[4,2,36,1024]{3,1,2,0:T(2,128)(2,1)S(1)} async-done(((bf16[4,2,36,1024]{3,1,2,0:T(2,128)(2,1)}), bf16[4,2,36,1024]{3,1,2,0:T(2,128)(2,1)S(1)}, u32[]{:S(2)}, u32[]{:S(2)}) %all-to-all-start.1) | async-done | bytes 589856 | tf_op jit(solution)/shard_map/all_to_all | solution.py:178
  239.2 3.5 %all-to-all-start.4 = ((bf16[2,4,2,36,1024]{4,2,3,0,1:T(2,128)(2,1)}), bf16[2,4,2,36,1024]{4,2,3,0,1:T(2,128)(2,1)S(1)}, u32[]{:S(2)}, u32[]{:S(2)}) async-start(bf16[2,4,2,36,1024]{4,2,3,0,1:T(2,128)(2,1)} %copy.86), calls=%async_computation.4 | async-start | bytes 2359296 | tf_op jit(solution)/shard_map/all_to_all | solution.py:209
  242.7 0.8 fusion.72
  243.8 2.1 fusion.60
  245.9 4.0 %collective-permute-start = (bf16[1,64,1024]{2,1,0:T(8,128)(2,1)}, bf16[1,64,1024]{2,1,0:T(8,128)(2,1)}, u32[]{:S(2)}, u32[]{:S(2)}) collective-permute-start(bf16[1,64,1024]{2,1,0:T(8,128)(2,1)} %fusion.60), channel_id=1, source_target_pairs={{0,8},{8,16},{16,24},{1,9},{9,17},{17,25},{2,10},{10,18},{18,26},{... | collective-permute-start | bytes 393224 | tf_op jit(solution)/shard_map/ppermute | solution.py:16
  249.9 8.6 %all-to-all-done.4 = bf16[2,4,2,36,1024]{4,2,3,0,1:T(2,128)(2,1)S(1)} async-done(((bf16[2,4,2,36,1024]{4,2,3,0,1:T(2,128)(2,1)}), bf16[2,4,2,36,1024]{4,2,3,0,1:T(2,128)(2,1)S(1)}, u32[]{:S(2)}, u32[]{:S(2)}) %all-to-all-start.4) | async-done | bytes 1179680 | tf_op jit(solution)/shard_map/all_to_all | solution.py:209
  258.5 0.8 fusion.117
  259.9 0.3 convolution_bitcast_fusion
  260.3 1.1 fusion.67
  261.5 0.6 multiply_reduce_fusion.2
  262.2 5.0 %all-reduce.2 = (f32[64,6]{0,1:T(8,128)S(1)}, f32[64,1]{0,1:T(1,128)S(1)}) all-reduce(f32[64,6]{0,1:T(8,128)S(1)} %bitcast.201, f32[64,1]{0,1:T(1,128)S(1)} %bitcast.202), channel_id=1, replica_groups=mesh['segment'=4,'expert'=4,'token'=2] {'token'}, use_global_device_ids=true, to_apply=%region_12.0 | all-reduce | flops 448 | bytes 3584 | tf_op jit(solution)/shard_map/psum | solution.py:221
  267.2 0.8 multiply_reduce_fusion
  268.2 1.3 collective-permute-start.1
  269.5 5.6 %collective-permute-done.1 = bf16[1,64,1024]{2,1,0:T(8,128)(2,1)S(1)} collective-permute-done((bf16[1,64,1024]{2,1,0:T(8,128)(2,1)S(1)}, bf16[1,64,1024]{2,1,0:T(8,128)(2,1)S(1)}, u32[]{:S(2)}, u32[]{:S(2)}) %collective-permute-start.1) | collective-permute-done | bytes 131104 | tf_op jit(solution)/shard_map/ppermute | solution.py:19
  275.0 1.6 copy.156
  276.6 0.7 copy.157
  (99 shorter events, 2.2 us)
Async XLA Ops:
  7.2 4.3 %copy-start = (f32[1,2048,8]{1,2,0:T(8,128)S(1)}, f32[1,2048,8]{1,2,0:T(8,128)}, u32[]{:S(2)}) copy-start(f32[1,2048,8]{1,2,0:T(8,128)} %param.20) | copy-start | bytes 196612
  9.3 7.1 %copy-start.13 = (pred[64,6]{0,1:T(8,128)(4,1)}, pred[64,6]{0,1:T(8,128)(4,1)S(1)}, u32[]{:S(2)}) copy-start(pred[64,6]{0,1:T(8,128)(4,1)S(1)} %bitcast_compare_fusion) | copy-start | bytes 1156
  10.4 3.2 %copy-start.17 = (f32[64]{0:T(128)}, f32[64]{0:T(128)S(1)}, u32[]{:S(2)}) copy-start(f32[64]{0:T(128)S(1)} %add_rsqrt_fusion) | copy-start | bytes 772
  11.5 9.2 %copy-start.5 = (bf16[1,64,2048]{2,1,0:T(8,128)(2,1)S(1)}, bf16[1,64,2048]{2,1,0:T(8,128)(2,1)}, u32[]{:S(2)}) copy-start(bf16[1,64,2048]{2,1,0:T(8,128)(2,1)} %param.18) | copy-start | bytes 786436
  13.6 7.1 %copy-start.15 = (f32[64]{0:T(128)}, f32[64]{0:T(128)S(1)}, u32[]{:S(2)}) copy-start(f32[64]{0:T(128)S(1)} %get-tuple-element.2) | copy-start | bytes 772
  15.0 7.7 %copy-start.11 = (s32[1,64,6]{1,0,2:T(1,128)S(1)}, s32[1,64,6]{1,0,2:T(1,128)}, u32[]{:S(2)}) copy-start(s32[1,64,6]{1,0,2:T(1,128)} %param.13) | copy-start | bytes 4612
  15.0 7.6 %copy-start.3 = (bf16[1,64,2048]{2,1,0:T(8,128)(2,1)S(1)}, bf16[1,64,2048]{2,1,0:T(8,128)(2,1)}, u32[]{:S(2)}) copy-start(bf16[1,64,2048]{2,1,0:T(8,128)(2,1)} %param.12) | copy-start | bytes 786436
  16.4 13.8 %all-to-all-start.2 = ((bf16[4,2,36,1024]{3,1,2,0:T(2,128)(2,1)}), bf16[4,2,36,1024]{3,1,2,0:T(2,128)(2,1)S(1)}, u32[]{:S(2)}, u32[]{:S(2)}) async-start(bf16[4,2,36,1024]{3,1,2,0:T(2,128)(2,1)} %copy.78), calls=%async_computation.2 | async-start | bytes 1179648 | tf_op jit(solution)/shard_map/all_to_all | solution.py:186
  21.0 13.8 %copy-start.8 = (f32[1,2048]{1,0:T(1,128)S(1)}, f32[1,2048]{1,0:T(1,128)}, u32[]{:S(2)}) copy-start(f32[1,2048]{1,0:T(1,128)} %param.19) | copy-start | bytes 24580
  21.2 14.1 %copy-start.12 = (s32[1,64,6]{1,0,2:T(1,128)S(1)}, s32[1,64,6]{1,0,2:T(1,128)}, u32[]{:S(2)}) copy-start(s32[1,64,6]{1,0,2:T(1,128)} %param.14) | copy-start | bytes 4612
  30.2 13.0 %all-to-all-start.3 = ((bf16[4,2,36,1024]{3,1,2,0:T(2,128)(2,1)}), bf16[4,2,36,1024]{3,1,2,0:T(2,128)(2,1)S(1)}, u32[]{:S(2)}, u32[]{:S(2)}) async-start(bf16[4,2,36,1024]{3,1,2,0:T(2,128)(2,1)} %copy.81), calls=%async_computation.3 | async-start | bytes 1179648 | tf_op jit(solution)/shard_map/all_to_all | solution.py:192
  33.7 49.6 %all-gather.6.cloned.1.call-start = ((), (), s32[]{:S(2)}) async-start(), calls=%async_computation.6 | async-start | bytes 1966080 | tf_op jit(solution)/shard_map/all_gather | solution.py:185
  34.8 53.7 %all-gather.8.cloned.1.call-start = ((), (), s32[]{:S(2)}) async-start(), calls=%async_computation.7 | async-start | bytes 1966080 | tf_op jit(solution)/shard_map/all_gather | solution.py:191
  47.1 35.0 %all-to-all-start = ((bf16[4,2,36,1024]{3,1,2,0:T(2,128)(2,1)}), bf16[4,2,36,1024]{3,1,2,0:T(2,128)(2,1)S(1)}, u32[]{:S(2)}, u32[]{:S(2)}) async-start(bf16[4,2,36,1024]{3,1,2,0:T(2,128)(2,1)} %copy.72), calls=%async_computation | async-start | bytes 1179648 | tf_op jit(solution)/shard_map/all_to_all | solution.py:166
  50.5 63.7 %all-gather.4.cloned.1.call-start = ((), (), s32[]{:S(2)}) async-start(), calls=%async_computation.5 | async-start | bytes 1966080 | tf_op jit(solution)/shard_map/all_gather | solution.py:165
  83.1 139.8 %all-reduce.6.cloned.1.call-start = ((), (), s32[]{:S(2)}) async-start(), calls=%async_computation.8 | async-start | bytes 7077888
  88.5 10.4 %slice-start = ((s8[5767168]{0:T(1024)(128)(4,1)}), s8[4194304]{0:T(1024)(128)(4,1)S(1)}, s32[]{:S(2)}) async-start(s8[5767168]{0:T(1024)(128)(4,1)} %bitcast.180), calls=%async_computation.9 | async-start | bytes 8388608
  88.5 12.3 %slice-start.2 = ((s8[5767168]{0:T(1024)(128)(4,1)}), s8[4194304]{0:T(1024)(128)(4,1)S(1)}, s32[]{:S(2)}) async-start(s8[5767168]{0:T(1024)(128)(4,1)} %bitcast.182), calls=%async_computation.11 | async-start | bytes 8388608
  93.5 5.3 %slice-start.1 = ((s8[5767168]{0:T(1024)(128)(4,1)}), s8[1572864]{0:T(1024)(128)(4,1)S(1)}, s32[]{:S(2)}) async-start(s8[5767168]{0:T(1024)(128)(4,1)} %bitcast.180), calls=%async_computation.10 | async-start | bytes 3145728
  93.6 5.3 %copy-start.1 = (bf16[4,2,36,2048]{3,2,0,1:T(8,128)(2,1)S(1)}, bf16[4,2,36,2048]{3,2,0,1:T(8,128)(2,1)}, u32[]{:S(2)}) copy-start(bf16[4,2,36,2048]{3,2,0,1:T(8,128)(2,1)} %all-gather.6.cloned.1.call-done) | copy-start | bytes 3538948
  93.6 7.2 %slice-start.3 = ((s8[5767168]{0:T(1024)(128)(4,1)}), s8[1572864]{0:T(1024)(128)(4,1)S(1)}, s32[]{:S(2)}) async-start(s8[5767168]{0:T(1024)(128)(4,1)} %bitcast.182), calls=%async_computation.12 | async-start | bytes 3145728
  98.9 4.4 %slice-start.6 = ((s8[5767168]{0:T(1024)(128)(4,1)}), s8[4194304]{0:T(1024)(128)(4,1)S(1)}, s32[]{:S(2)}) async-start(s8[5767168]{0:T(1024)(128)(4,1)} %bitcast.188), calls=%async_computation.15 | async-start | bytes 8388608
  100.8 2.4 slice-start.7
  114.3 5.1 %copy-start.4 = (bf16[4,2,36,2048]{3,2,0,1:T(8,128)(2,1)S(1)}, bf16[4,2,36,2048]{3,2,0,1:T(8,128)(2,1)}, u32[]{:S(2)}) copy-start(bf16[4,2,36,2048]{3,2,0,1:T(8,128)(2,1)} %all-gather.4.cloned.1.call-done) | copy-start | bytes 3538948
  114.3 9.8 %slice-start.4 = ((s8[5767168]{0:T(1024)(128)(4,1)}), s8[4194304]{0:T(1024)(128)(4,1)S(1)}, s32[]{:S(2)}) async-start(s8[5767168]{0:T(1024)(128)(4,1)} %bitcast.185), calls=%async_computation.13 | async-start | bytes 8388608
  119.4 4.7 %slice-start.5 = ((s8[5767168]{0:T(1024)(128)(4,1)}), s8[1572864]{0:T(1024)(128)(4,1)S(1)}, s32[]{:S(2)}) async-start(s8[5767168]{0:T(1024)(128)(4,1)} %bitcast.185), calls=%async_computation.14 | async-start | bytes 3145728
  126.3 2.0 copy-start.19
  226.2 13.0 %all-to-all-start.1 = ((bf16[4,2,36,1024]{3,1,2,0:T(2,128)(2,1)}), bf16[4,2,36,1024]{3,1,2,0:T(2,128)(2,1)S(1)}, u32[]{:S(2)}, u32[]{:S(2)}) async-start(bf16[4,2,36,1024]{3,1,2,0:T(2,128)(2,1)} %copy.76), calls=%async_computation.1 | async-start | bytes 1179648 | tf_op jit(solution)/shard_map/all_to_all | solution.py:178
  232.0 10.7 %copy-start.9 = (f32[1,2048]{1,0:T(1,128)S(1)}, f32[1,2048]{1,0:T(1,128)}, u32[]{:S(2)}) copy-start(f32[1,2048]{1,0:T(1,128)} %param.19) | copy-start | bytes 24580
  232.0 10.7 %copy-start.14 = (pred[64,6]{0,1:T(8,128)(4,1)S(1)}, pred[64,6]{0,1:T(8,128)(4,1)}, u32[]{:S(2)}) copy-start(pred[64,6]{0,1:T(8,128)(4,1)} %copy-done.13) | copy-start | bytes 1156
  239.2 19.3 %all-to-all-start.4 = ((bf16[2,4,2,36,1024]{4,2,3,0,1:T(2,128)(2,1)}), bf16[2,4,2,36,1024]{4,2,3,0,1:T(2,128)(2,1)S(1)}, u32[]{:S(2)}, u32[]{:S(2)}) async-start(bf16[2,4,2,36,1024]{4,2,3,0,1:T(2,128)(2,1)} %copy.86), calls=%async_computation.4 | async-start | bytes 2359296 | tf_op jit(solution)/shard_map/all_to_all | solution.py:209
  245.9 23.5 %collective-permute-start = (bf16[1,64,1024]{2,1,0:T(8,128)(2,1)}, bf16[1,64,1024]{2,1,0:T(8,128)(2,1)}, u32[]{:S(2)}, u32[]{:S(2)}) collective-permute-start(bf16[1,64,1024]{2,1,0:T(8,128)(2,1)} %fusion.60), channel_id=1, source_target_pairs={{0,8},{8,16},{16,24},{1,9},{9,17},{17,25},{2,10},{10,18},{18,26},{... | collective-permute-start | bytes 393224 | tf_op jit(solution)/shard_map/ppermute | solution.py:16
  259.3 1.0 copy-start.7
  259.5 2.0 copy-start.6
  259.6 7.6 %copy-start.16 = (f32[64]{0:T(128)S(1)}, f32[64]{0:T(128)}, u32[]{:S(2)}) copy-start(f32[64]{0:T(128)} %copy-done.15) | copy-start | bytes 772
  259.6 7.6 %copy-start.2 = (bf16[1,64,2048]{2,1,0:T(8,128)(2,1)S(1)}, bf16[1,64,2048]{2,1,0:T(8,128)(2,1)}, u32[]{:S(2)}) copy-start(bf16[1,64,2048]{2,1,0:T(8,128)(2,1)} %param.15) | copy-start | bytes 786436
  259.6 7.6 %copy-start.10 = (f32[1,2048]{1,0:T(1,128)S(1)}, f32[1,2048]{1,0:T(1,128)}, u32[]{:S(2)}) copy-start(f32[1,2048]{1,0:T(1,128)} %param.19) | copy-start | bytes 24580
  259.7 7.6 %copy-start.18 = (f32[64]{0:T(128)S(1)}, f32[64]{0:T(128)}, u32[]{:S(2)}) copy-start(f32[64]{0:T(128)} %copy-done.17) | copy-start | bytes 772
  268.2 6.9 %collective-permute-start.1 = (bf16[1,64,1024]{2,1,0:T(8,128)(2,1)S(1)}, bf16[1,64,1024]{2,1,0:T(8,128)(2,1)S(1)}, u32[]{:S(2)}, u32[]{:S(2)}) collective-permute-start(bf16[1,64,1024]{2,1,0:T(8,128)(2,1)S(1)} %fusion.91), channel_id=1, source_target_pairs={{8,0},{16,8},{24,16},{9,1},{17,9},{25,17},{10,2},{18,10},{26,18},{... | collective-permute-start | bytes 393224 | tf_op jit(solution)/shard_map/ppermute | solution.py:19
Sparse Core Ops, SparseCore 0:
  36.1 26.5 all-gather.5
  64.2 24.2 all-gather.7
  90.0 24.2 all-gather.3
  128.4 94.3 all-reduce.5
where the time goes:
time: 285 us; the launch traced here: 284 us
  waiting for transfers between devices  133 us (47%)
  local copies, waits for them, and re-layouts  58.5 us (21%)
  matrix products  41.8 us (15%)
  starting transfers between devices  23.9 us (8%)
  between operations  14.5 us (5%)
  other arithmetic  6.87 us (2%)
  blocking collectives  4.99 us (2%)
    unnamed x5, waiting for transfers between devices  94 us
    reshape x2, local copies, waits for them, and re-layouts, into_part(): rows_of.reshape(weight.shape[0], count, width_part, weight.shape[2])  21 us
    reshape x1, local copies, waits for them, and re-layouts, down_part(): columns.reshape(down_w.shape[0], down_w.shape[1], count, width_part)  10.5 us
    all_to_all x1, waiting for transfers between devices, body(): lax.all_to_all(summed[0].astype(jnp.bfloat16), 'expert', split_axis=1, co...  8.56 us
    convert_element_type x4, local copies, waits for them, and re-layouts, body(): summed[0].astype(jnp.bfloat16)  7.91 us
    all_to_all x1, waiting for transfers between devices, body(): lax.all_to_all(sent_c, 'expert', split_axis=0, concat_axis=0, tiled=True)  7.84 us
    dot_general x2, matrix products, into_part(): jnp.einsum('secf,enqf->nsecq', grads, rows_of, preferred_element_type=jnp...  7.79 us
    all_to_all x1, waiting for transfers between devices, body(): lax.all_to_all(sent_b, 'expert', split_axis=0, concat_axis=0, tiled=True)  7.43 us
  transfers between devices with their start and end apart: 11, of which 8 were waited for; matrix products, arithmetic and copies ran while one was open for 28% of the time, Pallas kernels for 0%

commit v1 on v0

v1 whole, which is shorter than its diff:
```python
import functools

import jax
import jax.numpy as jnp
from jax import lax
from jax.experimental import pallas as pl
from jax.experimental.pallas import tpu as pltpu
from jax.sharding import PartitionSpec as P

route_scale = 2.446
norm_eps = 1e-06
highest = lax.Precision.HIGHEST
MESH = pl.DeviceIdType.MESH
f32 = jnp.float32
bf16 = jnp.bfloat16
NT = (((1,), (1,)), ((), ()))
NN = (((1,), (0,)), ((), ()))


def mm(a, b, dims=NN):
    return lax.dot_general(a, b, dims, preferred_element_type=f32)


def kernel(
    sizes,
    fa,
    ba,
    bg,
    codes,
    gain,
    router_t,
    wg_h,
    wu_h,
    wd_h,
    out_next,
    out_prev,
    X,
    N,
    G,
    wg,
    wu,
    wd,
    gg,
    gu,
    Pb,
    R1,
    Q,
    R2,
    Z,
    R3,
    Sc,
    Sb,
    RS,
    DGT,
    own,
    zbuf,
    w_sem,
    l_sem,
    s0,
    r0,
    s1,
    r1,
    sg,
    rg,
    ssib,
    rsib,
    stok,
    rtok,
    sR1,
    rR1,
    sR2,
    rR2,
    sR3,
    rR3,
    sS,
    rS,
    sz,
    rz,
):
    n_seg, n_e, n_t, per, E, tok, D, F, K = sizes
    J = n_e // 2
    W = D // n_t
    T = n_e * tok
    seg = lax.axis_index("segment")
    me = lax.axis_index("expert")
    x = lax.axis_index("token")
    k = lax.rem(me, 2)
    j0 = me // 2
    sib = j0 * 2 + 1 - k

    def cols(share):
        return pl.ds(pl.multiple_of(share * W, 128), W)

    def rcopy(src, dst, ss, rs, dev):
        return pltpu.make_async_remote_copy(
            src_ref=src, dst_ref=dst, send_sem=ss, recv_sem=rs, device_id=dev, device_id_type=MESH
        )

    started = []

    def go(copy):
        copy.start()
        started.append(copy)
        return copy

    ins = (fa, ba, bg)
    local = []
    for s in range(3):
        c = pltpu.make_async_copy(ins[s].at[0], X.at[s, k, j0], l_sem.at[s])
        c.start()
        local.append(c)
    weights = []
    for i, (h, v) in enumerate(((wg_h, wg), (wu_h, wu), (wd_h, wd))):
        c = pltpu.make_async_copy(h, v, w_sem.at[i])
        c.start()
        weights.append(c)

    barrier = pltpu.get_barrier_semaphore()
    for de in range(n_e):
        for dt in range(n_t):
            if de or dt:
                pl.semaphore_signal(
                    barrier,
                    inc=1,
                    device_id={"expert": lax.rem(me + de, n_e), "token": lax.rem(x + dt, n_t)},
                    device_id_type=MESH,
                )

    @pl.when(seg > 0)
    def _():
        pl.semaphore_signal(barrier, inc=1, device_id={"segment": seg - 1}, device_id_type=MESH)

    @pl.when(seg < n_seg - 1)
    def _():
        pl.semaphore_signal(barrier, inc=1, device_id={"segment": seg + 1}, device_id_type=MESH)

    inner = jnp.where(seg > 0, 1, 0) + jnp.where(seg < n_seg - 1, 1, 0)
    pl.semaphore_wait(barrier, n_e * n_t - 1 + inner)

    c0 = []
    c1 = []
    for s in range(3):
        c1.append(
            [
                go(
                    rcopy(
                        ins[s].at[0, :, cols(x)],
                        X.at[s, k, j0, :, cols(x)],
                        s1.at[s, d - 1],
                        r1.at[s, d - 1],
                        {"expert": lax.rem(j0 + d, J) * 2 + k},
                    )
                )
                for d in range(1, J)
            ]
        )
        c0.append(go(rcopy(ins[s].at[0], X.at[s, k, j0], s0.at[s], r0.at[s], {"expert": sib})))

    def normed_block(s, raw):
        wide = raw.astype(f32)
        inverse = lax.rsqrt(jnp.mean(wide * wide, axis=-1, keepdims=True) + norm_eps)
        scaled = wide * inverse
        return (scaled * gain[...]).astype(bf16), inverse

    lane = lax.broadcasted_iota(jnp.int32, (tok, E), 1)

    def gating(normed, first):
        logits = lax.dot_general(
            normed.astype(f32), router_t[...], NT, precision=highest, preferred_element_type=f32
        )
        probs = jax.nn.sigmoid(logits)
        picked = jnp.zeros((tok, E), f32)
        kept = jnp.zeros((tok, E), f32)
        for c in range(K):
            code = codes[:, first + c : first + c + 1]
            held = (code == lane).astype(f32)
            kept += held
            picked += held + (code == lane + E).astype(f32)
        total = jnp.sum(picked * probs, axis=-1, keepdims=True)
        return logits, probs, picked, kept, total, kept * (route_scale * probs / total)

    for c in local:
        c.wait()
    normed_a, _ = normed_block(0, X[0, k, j0])
    gates_a = gating(normed_a, 0)[5]
    normed_b, inverse_b = normed_block(1, X[1, k, j0])
    logits_b, probs_b, picked_b, kept_b, total_b, gates_b = gating(normed_b, K)
    own[0, :, 0:E] = logits_b
    own[1, :, 0:E] = probs_b
    own[2, :, 0:E] = picked_b
    own[3, :, 0:E] = kept_b
    own[4, :, 0:E] = jnp.broadcast_to(total_b, (tok, E))
    own[5, :, 0:E] = jnp.broadcast_to(inverse_b, (tok, E))
    G[k, j0] = jnp.zeros((tok, 128), f32)
    G[k, j0, :, 0:E] = gates_a
    G[k, j0, :, E : 2 * E] = gates_b
    cg = [
        go(
            rcopy(
                G.at[k, j0],
                G.at[k, j0],
                sg.at[d - 1],
                rg.at[d - 1],
                {"expert": lax.rem(me + d, n_e)},
            )
        )
        for d in range(1, n_e)
    ]

    def relay_first(s):
        out = []
        for d in range(1, J):
            src = lax.rem(j0 - d + J, J)
            c1[s][d - 1].wait_recv()
            part = X.at[s, k, src, :, cols(x)]
            to_tok = [
                go(
                    rcopy(
                        part,
                        part,
                        stok.at[s, d - 1, t - 1],
                        rtok.at[s, d - 1, t - 1],
                        {"token": lax.rem(x + t, n_t)},
                    )
                )
                for t in range(1, n_t)
            ]
            to_sib = go(
                rcopy(part, part, ssib.at[s, d - 1, 0], rsib.at[s, d - 1, 0], {"expert": sib})
            )
            out.append((to_tok, to_sib))
        return out

    def relay_second(s, first):
        sibs = []
        for d in range(1, J):
            src = lax.rem(j0 - d + J, J)
            to_tok, to_sib = first[d - 1]
            sibs.append(to_sib)
            for t in range(1, n_t):
                to_tok[t - 1].wait_recv()
                part = X.at[s, k, src, :, cols(lax.rem(x - t + n_t, n_t))]
                sibs.append(
                    go(
                        rcopy(
                            part, part, ssib.at[s, d - 1, t], rsib.at[s, d - 1, t], {"expert": sib}
                        )
                    )
                )
        return sibs

    def arrive(s, sibs):
        c0[s].wait_recv()
        for c in sibs:
            c.wait_recv()

    def normalize_all(s):
        def step(i, carry):
            p = i // J
            j = lax.rem(i, J)
            N[p, j] = normed_block(s, X[s, p, j])[0]
            return carry

        lax.fori_loop(0, n_e, step, 0)

    def column(s, e):
        want = s * E + me * per + e
        lanes = lax.broadcasted_iota(jnp.int32, (T, 128), 1)
        return jnp.sum(jnp.where(lanes == want, G[...].reshape(T, 128), 0.0), axis=1, keepdims=True)

    tile = min(512, W)

    def produce(r, emit):
        copies = []
        for ti in list(range(1, n_t)) + [0]:
            share = lax.rem(x + ti, n_t)

            def step(n, carry):
                at = pl.multiple_of(share * W + n * tile, tile)
                value = emit(at).astype(bf16).reshape(2, J, tok, tile)
                Pb[r, ti, :, :, :, pl.ds(pl.multiple_of(n * tile, tile), tile)] = value
                return carry

            lax.fori_loop(0, W // tile, step, 0)
            copies.append(
                go(
                    rcopy(
                        Pb.at[r, ti, 1 - k],
                        R1.at[r, ti],
                        sR1.at[r, ti],
                        rR1.at[r, ti],
                        {"expert": sib},
                    )
                )
            )
        return copies

    def pair_sum(r, ti):
        return Pb[r, ti, k].astype(f32) + R1[r, ti].astype(f32)

    def exchange(r, copies):
        sent = []
        for ti in range(1, n_t):
            copies[ti - 1].wait_recv()
            Q[r, ti - 1] = pair_sum(r, ti).astype(bf16)
            sent.append(
                go(
                    rcopy(
                        Q.at[r, ti - 1],
                        R2.at[r, ti - 1],
                        sR2.at[r, ti - 1],
                        rR2.at[r, ti - 1],
                        {"token": lax.rem(x + ti, n_t)},
                    )
                )
            )
        copies[n_t - 1].wait_recv()
        return sent

    def cross(r, sent):
        for c in sent:
            c.wait_recv()
        total = pair_sum(r, 0)
        for ti in range(1, n_t):
            total += R2[r, ti - 1].astype(f32)
        Z[r] = total.astype(bf16)
        return [
            go(
                rcopy(
                    Z.at[r, lax.rem(j0 + d, J)],
                    R3.at[r, d - 1],
                    sR3.at[r, d - 1],
                    rR3.at[r, d - 1],
                    {"expert": lax.rem(j0 + d, J) * 2 + k},
                )
            )
            for d in range(1, J)
        ]

    def gathered(r, sent):
        for c in sent:
            c.wait_recv()
        total = Z[r, j0].astype(f32)
        for d in range(1, J):
            total += R3[r, d - 1].astype(f32)
        return total

    first_a = relay_first(0)
    sibs_a = relay_second(0, first_a)
    arrive(0, sibs_a)
    normalize_all(0)
    weights[0].wait()
    weights[1].wait()
    for c in cg:
        c.wait_recv()

    first_b = relay_first(1)

    def fwd_step(e, carry):
        rows = N[...].reshape(T, D)
        gate = mm(rows, wg[e], NT)
        up = mm(rows, wu[e], NT)
        gg[e] = (gate * jax.nn.sigmoid(gate) * up * column(0, e)).astype(bf16)
        return carry

    lax.fori_loop(0, per, fwd_step, 0)
    weights[2].wait()
    first_c = relay_first(2)
    sibs_b = relay_second(1, first_b)

    def emit_fwd(at):
        total = mm(gg[0], wd[0, :, pl.ds(at, tile)])
        for e in range(1, per):
            total += mm(gg[e], wd[e, :, pl.ds(at, tile)])
        return total

    p_fwd = produce(0, emit_fwd)
    sibs_c = relay_second(2, first_c)
    sent_fwd = exchange(0, p_fwd)
    arrive(1, sibs_b)
    arrive(2, sibs_c)
    normalize_all(1)
    Sc[...] = jnp.zeros((T, 128), f32)

    def bwd_step(e, carry):
        rows = N[...].reshape(T, D)
        gate = mm(rows, wg[e], NT)
        up = mm(rows, wu[e], NT)
        grad_act = mm(X[2].reshape(T, D), wd[e], NT)
        sigma = jax.nn.sigmoid(gate)
        silu = gate * sigma
        ggv = grad_act * up * sigma * (1.0 + gate * (1.0 - sigma))
        guv = grad_act * silu
        col = column(1, e)
        dg = jnp.sum(guv * up, axis=1, keepdims=True)
        corr = col * jnp.sum(ggv * gate + guv * up, axis=1, keepdims=True)
        lanes = lax.broadcasted_iota(jnp.int32, (T, 128), 1)
        Sc[...] += jnp.where(lanes == e, dg, 0.0) + jnp.where(lanes == per, corr, 0.0)
        gg[e] = (ggv * col).astype(bf16)
        gu[e] = (guv * col).astype(bf16)
        return carry

    lax.fori_loop(0, per, bwd_step, 0)
    cross_fwd = cross(0, sent_fwd)

    flipped = jnp.transpose(Sc[...])[0:8]
    for p in range(2):
        for j in range(J):
            at = (p * J + j) * tok
            Sb[j * 2 + p] = flipped[:, at : at + tok]
    cs = []
    for de in range(n_e):
        for dt in range(n_t):
            if de or dt:
                to = lax.rem(me + de, n_e)
                cs.append(
                    go(
                        rcopy(
                            Sb.at[to],
                            RS.at[me, x],
                            sS.at[de, dt],
                            rS.at[de, dt],
                            {"expert": to, "token": lax.rem(x + dt, n_t)},
                        )
                    )
                )
    RS[me, x] = Sb[me]

    def emit_bwd(at):
        total = None
        for e in range(per):
            for grads, w in ((gg, wg), (gu, wu)):
                piece = mm(grads[e], w[e, :, pl.ds(at, tile)])
                total = piece if total is None else total + piece
        return total

    p_bwd = produce(1, emit_bwd)

    next_rows = X[0, k, j0, :, cols(x)].astype(f32) + gathered(0, cross_fwd)
    zbuf[0] = next_rows.astype(bf16)

    def send_next():
        return rcopy(
            zbuf.at[0], out_next.at[0], sz.at[0], rz.at[0], {"segment": lax.rem(seg + 1, n_seg)}
        )

    def send_prev():
        return rcopy(
            zbuf.at[1],
            out_prev.at[0],
            sz.at[1],
            rz.at[1],
            {"segment": lax.rem(seg - 1 + n_seg, n_seg)},
        )

    @pl.when(seg < n_seg - 1)
    def _():
        send_next().start()

    @pl.when(seg == 0)
    def _():
        out_next[...] = jnp.zeros(out_next.shape, bf16)

    @pl.when(seg == n_seg - 1)
    def _():
        out_prev[...] = jnp.zeros(out_prev.shape, bf16)

    sent_bwd = exchange(1, p_bwd)

    for c in cs:
        c.wait_recv()
    DGT[...] = jnp.zeros(DGT.shape, f32)
    corr = jnp.zeros((1, tok), f32)
    for e in range(n_e):
        total = RS[e, 0]
        for t in range(1, n_t):
            total += RS[e, t]
        DGT[e * per : (e + 1) * per, 0:tok] = total[0:per]
        corr += total[per : per + 1]
    DGT[E : E + 1, 0:tok] = corr
    turned = jnp.transpose(DGT[...])[0:tok]
    logits_b = own[0, :, 0:E]
    probs_b = own[1, :, 0:E]
    total_b = own[4, :, 0:E]
    inverse_b = own[5, :, 0:1]
    dgates = jnp.where(own[3, :, 0:E] > 0.5, turned[:, 0:E], 0.0)
    spread = jnp.sum(dgates * probs_b, axis=-1, keepdims=True)
    dprobs = route_scale * dgates / total_b - route_scale * spread / (total_b * total_b)
    dlogits = jnp.where(own[2, :, 0:E] > 0.5, dprobs * probs_b * (1.0 - probs_b), 0.0)
    mean_all = (turned[:, E : E + 1] + jnp.sum(dlogits * logits_b, axis=-1, keepdims=True)) / D
    router_own = lax.dot_general(
        dlogits, router_t[:, cols(x)], NN, precision=highest, preferred_element_type=f32
    )
    gain_own = gain[:, cols(x)]
    scaled_own = X[1, k, j0, :, cols(x)].astype(f32) * inverse_b
    cot_own = X[2, k, j0, :, cols(x)].astype(f32)
    base = cot_own + inverse_b * (router_own * gain_own - scaled_own * mean_all)

    cross_bwd = cross(1, sent_bwd)
    zbuf[1] = (base + inverse_b * gain_own * gathered(1, cross_bwd)).astype(bf16)

    @pl.when(seg > 0)
    def _():
        send_prev().start()

    for c in started:
        c.wait_send()

    @pl.when(seg < n_seg - 1)
    def _():
        send_next().wait_send()
        send_prev().wait_recv()

    @pl.when(seg > 0)
    def _():
        send_prev().wait_send()
        send_next().wait_recv()


def body(
    fwd_acts,
    fwd_ids,
    fwd_slots,
    bwd_acts,
    bwd_ids,
    bwd_slots,
    bwd_grad,
    norm_gain,
    router,
    w_gate,
    w_up,
    w_down,
):
    E = router.shape[2]
    per, D, F = w_gate.shape
    n_seg = lax.axis_size("segment")
    n_e = lax.axis_size("expert")
    n_t = lax.axis_size("token")
    tok = fwd_acts.shape[1]
    K = fwd_ids.shape[2]
    cap = max(2, min(3 * tok * K // (4 * E), tok - 1))
    W = D // n_t
    J = n_e // 2
    T = n_e * tok
    V = pltpu.VMEM
    dma = pltpu.SemaphoreType.DMA
    peers = max(J - 1, 1)
    toks = max(n_t - 1, 1)
    scratch = [
        V((3, 2, J, tok, D), bf16),
        V((2, J, tok, D), bf16),
        V((2, J, tok, 128), f32),
        V((per, F, D), bf16),
        V((per, F, D), bf16),
        V((per, F, D), bf16),
        V((per, T, F), bf16),
        V((per, T, F), bf16),
        V((2, n_t, 2, J, tok, W), bf16),
        V((2, n_t, J, tok, W), bf16),
        V((2, toks, J, tok, W), bf16),
        V((2, toks, J, tok, W), bf16),
        V((2, J, tok, W), bf16),
        V((2, peers, tok, W), bf16),
        V((T, 128), f32),
        V((n_e, 8, tok), f32),
        V((n_e, n_t, 8, tok), f32),
        V((128, 128), f32),
        V((6, tok, 128), f32),
        V((2, tok, W), bf16),
        dma((3,)),
        dma((3,)),
        dma((3,)),
        dma((3,)),
        dma((3, peers)),
        dma((3, peers)),
        dma((n_e - 1,)),
        dma((n_e - 1,)),
        dma((3, peers, n_t)),
        dma((3, peers, n_t)),
        dma((3, peers, toks)),
        dma((3, peers, toks)),
        dma((2, n_t)),
        dma((2, n_t)),
        dma((2, toks)),
        dma((2, toks)),
        dma((2, peers)),
        dma((2, peers)),
        dma((n_e, n_t)),
        dma((n_e, n_t)),
        dma((2,)),
        dma((2,)),
    ]
    codes = jnp.concatenate(
        [
            ids[0] + jnp.where(slots[0] < cap, 0, E)
            for ids, slots in ((fwd_ids, fwd_slots), (bwd_ids, bwd_slots))
        ],
        axis=1,
    )
    vm = pl.BlockSpec(memory_space=pltpu.VMEM)
    hbm = pl.BlockSpec(memory_space=pl.ANY)
    out = jax.ShapeDtypeStruct((1, tok, W), bf16)
    sizes = (n_seg, n_e, n_t, per, E, tok, D, F, K)
    return pl.pallas_call(
        functools.partial(kernel, sizes),
        out_shape=(out, out),
        in_specs=[hbm] * 3 + [vm] * 3 + [hbm] * 3,
        out_specs=(vm, vm),
        scratch_shapes=scratch,
        compiler_params=pltpu.CompilerParams(
            collective_id=0, has_side_effects=True, vmem_limit_bytes=63 * 1024 * 1024
        ),
        name="relay_moe",
    )(
        fwd_acts,
        bwd_acts,
        bwd_grad,
        codes,
        norm_gain,
        router[0].T,
        jnp.swapaxes(w_gate, 1, 2),
        jnp.swapaxes(w_up, 1, 2),
        w_down,
    )


def solution(mesh):
    return jax.shard_map(
        body,
        mesh=mesh,
        in_specs=(
            P("segment", "expert", None),
            P("segment", "expert", None),
            P("segment", "expert", None),
            P("segment", "expert", None),
            P("segment", "expert", None),
            P("segment", "expert", None),
            P("segment", "expert", None),
            P("segment", None),
            P("segment", None, None),
            P("expert", None, "token"),
            P("expert", None, "token"),
            P("expert", "token", None),
        ),
        out_specs=(P("segment", "expert", "token"), P("segment", "expert", "token")),
        check_vma=False,
    )
```

time: 285 us -> 61.1 us (0.21)
  waiting for transfers between devices: 133 us -> 0 us
  Pallas kernels: 0 us -> 55.7 us
  local copies, waits for them, and re-layouts: 58.5 us -> 3.85 us
  matrix products: 41.8 us -> 0 us
  starting transfers between devices: 23.9 us -> 0 us
  between operations: 14.5 us -> 0.64 us
  other arithmetic: 6.87 us -> 0.75 us
  blocking collectives: 4.99 us -> 0 us
    unnamed x5 -> x0, waiting for transfers between devices: 94 us -> none
    pallas_call x0 -> x1, Pallas kernels: none -> 55.7 us  [body(): pl.pallas_call(functools.partial(kernel, sizes), out_shape=(out, out), in...]
    dot_general x19 -> x0, matrix products: 41.8 us -> none  [the longest x2 7.79 us: into_part(): jnp.einsum('secf,enqf->nsecq', grads, rows_of, preferred_element_type=jnp...]
    reshape x10 -> x0, local copies, waits for them, and re-layouts: 36.2 us -> none  [the longest x2 21 us: into_part(): rows_of.reshape(weight.shape[0], count, width_part, weight.shape[2])]
    all_to_all x5 -> x0, waiting for transfers between devices: 28.7 us -> none  [the longest x1 8.56 us: body(): lax.all_to_all(summed[0].astype(jnp.bfloat16), 'expert', split_axis=1, co...]
    all_to_all x5 -> x0, starting transfers between devices: 18.2 us -> none  [the longest x1 4.27 us: body(): lax.all_to_all(sent_b, 'expert', split_axis=0, concat_axis=0, tiled=True)]
    convert_element_type x5 -> x0, local copies, waits for them, and re-layouts: 9.85 us -> none  [the longest x4 7.91 us: body(): summed[0].astype(jnp.bfloat16)]
    ppermute x2 -> x0, waiting for transfers between devices: 5.55 us -> none  [the longest x1 5.55 us: extended(): lax.ppermute(lax.slice_in_dim(block, 0, width, axis=dim), axis, backward)]
  transfers between devices with their start and end apart: 11 -> 0, of which waited for: 8 -> 0; matrix products, arithmetic and copies ran while one was open for 28% -> 0% of each run, Pallas kernels for 0% -> 0%
where the time goes in v1:
time: 61.1 us; the launch traced here: 60.9 us
  Pallas kernels  55.7 us (91%)
  local copies, waits for them, and re-layouts  3.85 us (6%)
  other arithmetic  0.75 us (1%)
  between operations  0.64 us (1%)
    pallas_call x1, Pallas kernels, body(): pl.pallas_call(functools.partial(kernel, sizes), out_shape=(out, out), in...  55.7 us
    unnamed x2, local copies, waits for them, and re-layouts  3.14 us

profile of v1, /device:TPU:0, one launch (start us, length us, event | category | flops | bytes accessed | tf_op | source)
XLA Modules:
  0.0 60.9 jit_solution(2202092948020316644)
XLA Ops:
  0.6 0.7 %fusion = (s32[64,6]{0,1:T(8,128)S(1)}, s32[64,6]{0,1:T(8,128)S(1)}) fusion(s32[1,64,6]{1,0,2:T(1,128)} %param.16, s32[1,64,6]{1,0,2:T(1,128)} %param.17, s32[1,64,6]{1,0,2:T(1,128)} %param.14, s32[1,64,6]{1,0,2:T(1,128)} %param.13), kind=kLoop, calls=%fused_computation.2 | loop fusion | flops 2304 | bytes 9216 | tf_op jit(solution)/shard_map/add | solution.py:595
  1.4 0.7 %copy.28.codes = s32[64,12]{1,0:T(8,128)} copy(s32[64,12]{0,1:T(8,128)S(1)} %pad_add_fusion) | data formatting | bytes 6144 | tf_op jit(solution)/shard_map/concatenate | solution.py:593
  2.1 55.7 %relay_moe.1 = (bf16[1,64,1024]{2,1,0:T(8,128)(2,1)}, bf16[1,64,1024]{2,1,0:T(8,128)(2,1)}) custom-call(bf16[1,64,2048]{2,1,0:T(8,128)(2,1)} %fa.1, bf16[1,64,2048]{2,1,0:T(8,128)(2,1)} %ba.1, bf16[1,64,2048]{2,1,0:T(8,128)(2,1)} %bg.1, s32[64,12]{1,0:T(8,128)} %copy.28.codes, f32[1,2048]{1,0:T(1,128)} %gain.1, f32[8,2048]{1,0:T(8,128)} %bitcast.11, ...), custom_call_target="tpu_custom_call" | custom-call | tf_op jit(solution)/shard_map/relay_moe/pallas_call | solution.py:604
  57.8 1.6 %copy.43 = bf16[1,64,1024]{2,1,0:T(8,128)(2,1)} copy(bf16[1,64,1024]{2,1,0:T(8,128)(2,1)} %get-tuple-element.6) | data formatting | bytes 262144
  59.3 1.6 %copy.44 = bf16[1,64,1024]{2,1,0:T(8,128)(2,1)} copy(bf16[1,64,1024]{2,1,0:T(8,128)(2,1)} %get-tuple-element.7) | data formatting | bytes 262144
  (1 shorter events, 0.0 us)

commit v2 on v1

--- a/solution.py
+++ b/solution.py
@@ -40,20 +40,27 @@
     wg,
     wu,
     wd,
+    act,
     gg,
     gu,
     Pb,
     R1,
-    Q,
-    R2,
-    Z,
-    R3,
+    QA,
+    R2A,
+    ZA,
+    R3A,
+    QB,
+    R2B,
+    ZB,
+    R3B,
     Sc,
     Sb,
     RS,
     DGT,
     own,
+    own_base,
     zbuf,
+    turn,
     w_sem,
     l_sem,
     s0,
@@ -68,10 +75,14 @@
     rtok,
     sR1,
     rR1,
-    sR2,
-    rR2,
-    sR3,
-    rR3,
+    sR2A,
+    rR2A,
+    sR3A,
+    rR3A,
+    sR2B,
+    rR2B,
+    sR3B,
+    rR3B,
     sS,
     rS,
     sz,
@@ -109,11 +120,12 @@
         c = pltpu.make_async_copy(ins[s].at[0], X.at[s, k, j0], l_sem.at[s])
         c.start()
         local.append(c)
-    weights = []
-    for i, (h, v) in enumerate(((wg_h, wg), (wu_h, wu), (wd_h, wd))):
-        c = pltpu.make_async_copy(h, v, w_sem.at[i])
+    weights = [[], [], []]
+    pairs = [(i, e) for e in range(per) for i in (0, 1)] + [(2, e) for e in range(per)]
+    for i, e in pairs:
+        c = pltpu.make_async_copy(((wg_h, wu_h, wd_h)[i]).at[e], (wg, wu, wd)[i].at[e], w_sem.at[i, e])
         c.start()
-        weights.append(c)
+        weights[i].append(c)
 
     barrier = pltpu.get_barrier_semaphore()
     for de in range(n_e):
@@ -163,6 +175,9 @@
         return (scaled * gain[...]).astype(bf16), inverse
 
     lane = lax.broadcasted_iota(jnp.int32, (tok, E), 1)
+    turn[...] = jnp.zeros((128, 128), f32)
+    turn[0 : 2 * K, 0:tok] = codes[...].astype(f32)
+    codes_f = jnp.transpose(turn[...])[0:tok].astype(jnp.int32)
 
     def gating(normed, first):
         logits = lax.dot_general(
@@ -172,7 +187,7 @@
         picked = jnp.zeros((tok, E), f32)
         kept = jnp.zeros((tok, E), f32)
         for c in range(K):
-            code = codes[:, first + c : first + c + 1]
+            code = codes_f[:, first + c : first + c + 1]
             held = (code == lane).astype(f32)
             kept += held
             picked += held + (code == lane + E).astype(f32)
@@ -254,156 +269,251 @@
         for c in sibs:
             c.wait_recv()
 
-    def normalize_all(s):
-        def step(i, carry):
-            p = i // J
-            j = lax.rem(i, J)
+    def normalize(s, j):
+        for p in range(2):
             N[p, j] = normed_block(s, X[s, p, j])[0]
-            return carry
-
-        lax.fori_loop(0, n_e, step, 0)
-
-    def column(s, e):
+
+    M = 2 * tok
+    wide_lane = lax.broadcasted_iota(jnp.int32, (M, 128), 1)
+
+    def column(s, e, j):
         want = s * E + me * per + e
-        lanes = lax.broadcasted_iota(jnp.int32, (T, 128), 1)
-        return jnp.sum(jnp.where(lanes == want, G[...].reshape(T, 128), 0.0), axis=1, keepdims=True)
-
-    tile = min(512, W)
-
-    def produce(r, emit):
-        copies = []
-        for ti in list(range(1, n_t)) + [0]:
-            share = lax.rem(x + ti, n_t)
-
-            def step(n, carry):
-                at = pl.multiple_of(share * W + n * tile, tile)
-                value = emit(at).astype(bf16).reshape(2, J, tok, tile)
-                Pb[r, ti, :, :, :, pl.ds(pl.multiple_of(n * tile, tile), tile)] = value
-                return carry
-
-            lax.fori_loop(0, W // tile, step, 0)
-            copies.append(
-                go(
-                    rcopy(
-                        Pb.at[r, ti, 1 - k],
-                        R1.at[r, ti],
-                        sR1.at[r, ti],
-                        rR1.at[r, ti],
-                        {"expert": sib},
-                    )
-                )
-            )
-        return copies
-
-    def pair_sum(r, ti):
-        return Pb[r, ti, k].astype(f32) + R1[r, ti].astype(f32)
-
-    def exchange(r, copies):
-        sent = []
-        for ti in range(1, n_t):
-            copies[ti - 1].wait_recv()
-            Q[r, ti - 1] = pair_sum(r, ti).astype(bf16)
-            sent.append(
-                go(
-                    rcopy(
-                        Q.at[r, ti - 1],
-                        R2.at[r, ti - 1],
-                        sR2.at[r, ti - 1],
-                        rR2.at[r, ti - 1],
-                        {"token": lax.rem(x + ti, n_t)},
-                    )
-                )
-            )
-        copies[n_t - 1].wait_recv()
-        return sent
-
-    def cross(r, sent):
-        for c in sent:
-            c.wait_recv()
-        total = pair_sum(r, 0)
-        for ti in range(1, n_t):
-            total += R2[r, ti - 1].astype(f32)
-        Z[r] = total.astype(bf16)
-        return [
-            go(
-                rcopy(
-                    Z.at[r, lax.rem(j0 + d, J)],
-                    R3.at[r, d - 1],
-                    sR3.at[r, d - 1],
-                    rR3.at[r, d - 1],
-                    {"expert": lax.rem(j0 + d, J) * 2 + k},
-                )
-            )
-            for d in range(1, J)
-        ]
-
-    def gathered(r, sent):
-        for c in sent:
-            c.wait_recv()
-        total = Z[r, j0].astype(f32)
-        for d in range(1, J):
-            total += R3[r, d - 1].astype(f32)
-        return total
-
-    first_a = relay_first(0)
-    sibs_a = relay_second(0, first_a)
-    arrive(0, sibs_a)
-    normalize_all(0)
-    weights[0].wait()
-    weights[1].wait()
-    for c in cg:
-        c.wait_recv()
-
-    first_b = relay_first(1)
-
-    def fwd_step(e, carry):
-        rows = N[...].reshape(T, D)
+        picked = jnp.where(wide_lane == want, G[:, j].reshape(M, 128), 0.0)
+        return jnp.sum(picked, axis=1, keepdims=True)
+
+    def put(ref, e, j, value):
+        ref[e, :, j] = value.astype(bf16).reshape(2, tok, F)
+
+    def fwd_part(e, j):
+        rows = N[:, j].reshape(M, D)
         gate = mm(rows, wg[e], NT)
         up = mm(rows, wu[e], NT)
-        gg[e] = (gate * jax.nn.sigmoid(gate) * up * column(0, e)).astype(bf16)
-        return carry
-
-    lax.fori_loop(0, per, fwd_step, 0)
-    weights[2].wait()
-    first_c = relay_first(2)
-    sibs_b = relay_second(1, first_b)
-
-    def emit_fwd(at):
-        total = mm(gg[0], wd[0, :, pl.ds(at, tile)])
-        for e in range(1, per):
-            total += mm(gg[e], wd[e, :, pl.ds(at, tile)])
-        return total
-
-    p_fwd = produce(0, emit_fwd)
-    sibs_c = relay_second(2, first_c)
-    sent_fwd = exchange(0, p_fwd)
-    arrive(1, sibs_b)
-    arrive(2, sibs_c)
-    normalize_all(1)
-    Sc[...] = jnp.zeros((T, 128), f32)
-
-    def bwd_step(e, carry):
-        rows = N[...].reshape(T, D)
+        put(act, e, j, gate * jax.nn.sigmoid(gate) * up * column(0, e, j))
+
+    def bwd_part(e, j):
+        rows = N[:, j].reshape(M, D)
         gate = mm(rows, wg[e], NT)
         up = mm(rows, wu[e], NT)
-        grad_act = mm(X[2].reshape(T, D), wd[e], NT)
+        grad_act = mm(X[2, :, j].reshape(M, D), wd[e], NT)
         sigma = jax.nn.sigmoid(gate)
         silu = gate * sigma
         ggv = grad_act * up * sigma * (1.0 + gate * (1.0 - sigma))
         guv = grad_act * silu
-        col = column(1, e)
+        col = column(1, e, j)
         dg = jnp.sum(guv * up, axis=1, keepdims=True)
         corr = col * jnp.sum(ggv * gate + guv * up, axis=1, keepdims=True)
-        lanes = lax.broadcasted_iota(jnp.int32, (T, 128), 1)
-        Sc[...] += jnp.where(lanes == e, dg, 0.0) + jnp.where(lanes == per, corr, 0.0)
-        gg[e] = (ggv * col).astype(bf16)
-        gu[e] = (guv * col).astype(bf16)
-        return carry
-
-    lax.fori_loop(0, per, bwd_step, 0)
-    cross_fwd = cross(0, sent_fwd)
-
-    flipped = jnp.transpose(Sc[...])[0:8]
+        both = jnp.where(wide_lane == e, dg, 0.0) + jnp.where(wide_lane == per, corr, 0.0)
+        both = both.reshape(2, tok, 128)
+        Sc[:, j] = both if e == 0 else Sc[:, j] + both
+        put(gg, e, j, ggv * col)
+        put(gu, e, j, guv * col)
+
+    def others(fn):
+        if J == 2:
+            fn(1 - j0)
+        elif J > 2:
+
+            def step(d, carry):
+                fn(lax.rem(j0 + d, J))
+                return carry
+
+            lax.fori_loop(1, J, step, 0)
+
+    H = W // 2
+
+    def produce(r, h, emit):
+        def step(n, carry):
+            ti = lax.rem(n + 1, n_t)
+            at = pl.multiple_of(lax.rem(x + ti, n_t) * W + h * H, H)
+            Pb[r, h, :, ti] = emit(at).astype(bf16).reshape(2, J, tok, H)
+            return carry
+
+        lax.fori_loop(0, n_t, step, 0)
+        return go(
+            rcopy(Pb.at[r, h, 1 - k], R1.at[r, h], sR1.at[r, h], rR1.at[r, h], {"expert": sib})
+        )
+
+    def token_first(r, copy):
+        copy.wait_recv()
+        sent = []
+        for ti in range(1, n_t):
+            QA[r, ti - 1] = (Pb[r, 0, k, ti].astype(f32) + R1[r, 0, ti].astype(f32)).astype(bf16)
+            sent.append(
+                go(
+                    rcopy(
+                        QA.at[r, ti - 1],
+                        R2A.at[r, ti - 1],
+                        sR2A.at[r, ti - 1],
+                        rR2A.at[r, ti - 1],
+                        {"token": lax.rem(x + ti, n_t)},
+                    )
+                )
+            )
+        return sent
+
+    def expert_first(r, copy):
+        copy.wait_recv()
+        sent = []
+        for d in range(1, J):
+            jd = lax.rem(j0 + d, J)
+            total = Pb[r, 1, k, :, jd].astype(f32) + R1[r, 1, :, jd].astype(f32)
+            QB[r, d - 1] = total.astype(bf16)
+            sent.append(
+                go(
+                    rcopy(
+                        QB.at[r, d - 1],
+                        R2B.at[r, d - 1],
+                        sR2B.at[r, d - 1],
+                        rR2B.at[r, d - 1],
+                        {"expert": jd * 2 + k},
+                    )
+                )
+            )
+        return sent
+
+    def then_expert(r, sent):
+        for c in sent:
+            c.wait_recv()
+        total = Pb[r, 0, k, 0].astype(f32) + R1[r, 0, 0].astype(f32)
+        for ti in range(1, n_t):
+            total += R2A[r, ti - 1].astype(f32)
+        ZA[r] = total.astype(bf16)
+        return [
+            go(
+                rcopy(
+                    ZA.at[r, lax.rem(j0 + d, J)],
+                    R3A.at[r, d - 1],
+                    sR3A.at[r, d - 1],
+                    rR3A.at[r, d - 1],
+                    {"expert": lax.rem(j0 + d, J) * 2 + k},
+                )
+            )
+            for d in range(1, J)
+        ]
+
+    def then_token(r, sent):
+        for c in sent:
+            c.wait_recv()
+        total = Pb[r, 1, k, :, j0].astype(f32) + R1[r, 1, :, j0].astype(f32)
+        for d in range(1, J):
+            total += R2B[r, d - 1].astype(f32)
+        ZB[r] = total.astype(bf16)
+        return [
+            go(
+                rcopy(
+                    ZB.at[r, ti],
+                    R3B.at[r, ti - 1],
+                    sR3B.at[r, ti - 1],
+                    rR3B.at[r, ti - 1],
+                    {"token": lax.rem(x + ti, n_t)},
+                )
+            )
+            for ti in range(1, n_t)
+        ]
+
+    def last_a(r, sent):
+        for c in sent:
+            c.wait_recv()
+        total = ZA[r, j0].astype(f32)
+        for d in range(1, J):
+            total += R3A[r, d - 1].astype(f32)
+        return total
+
+    def last_b(r, sent):
+        for c in sent:
+            c.wait_recv()
+        total = ZB[r, 0].astype(f32)
+        for ti in range(1, n_t):
+            total += R3B[r, ti - 1].astype(f32)
+        return total
+
+    def half_cols(h):
+        return pl.ds(pl.multiple_of(x * W + h * H, 128), H)
+
+    def send_next(h):
+        part = (0, slice(None), pl.ds(h * H, H))
+        return rcopy(
+            zbuf.at[part],
+            out_next.at[part],
+            sz.at[0, h],
+            rz.at[0, h],
+            {"segment": lax.rem(seg + 1, n_seg)},
+        )
+
+    def send_prev(h):
+        part = (slice(None), pl.ds(h * H, H))
+        return rcopy(
+            zbuf.at[(1,) + part],
+            out_prev.at[(0,) + part],
+            sz.at[1, h],
+            rz.at[1, h],
+            {"segment": lax.rem(seg - 1 + n_seg, n_seg)},
+        )
+
+    def emit_fwd(at):
+        total = None
+        for e in range(per):
+            piece = mm(act[e].reshape(T, F), wd[e, :, pl.ds(at, H)])
+            total = piece if total is None else total + piece
+        return total
+
+    def emit_bwd(at):
+        total = None
+        for e in range(per):
+            for grads, w in ((gg, wg), (gu, wu)):
+                piece = mm(grads[e].reshape(T, F), w[e, :, pl.ds(at, H)])
+                total = piece if total is None else total + piece
+        return total
+
+    def finish_next(h, mixed):
+        rows = X[0, k, j0, :, half_cols(h)].astype(f32) + mixed
+        zbuf[0, :, h * H : (h + 1) * H] = rows.astype(bf16)
+
+        @pl.when(seg < n_seg - 1)
+        def _():
+            send_next(h).start()
+
+    c0[0].wait_recv()
+    normalize(0, j0)
+    for c in cg:
+        c.wait_recv()
+    for e in range(per):
+        weights[0][e].wait()
+        weights[1][e].wait()
+        fwd_part(e, j0)
+        if e == 0:
+            first_a = relay_first(0)
+    c0[1].wait_recv()
+    c0[2].wait_recv()
+    normalize(1, j0)
+    for e in range(per):
+        weights[2][e].wait()
+        bwd_part(e, j0)
+        if e == 0:
+            first_b = relay_first(1)
+    sibs_a = relay_second(0, first_a)
+    for c in sibs_a:
+        c.wait_recv()
+    others(lambda j: normalize(0, j))
+    others(lambda j: fwd_part(0, j))
+    first_c = relay_first(2)
+    sibs_b = relay_second(1, first_b)
+    for e in range(1, per):
+        others(functools.partial(fwd_part, e))
+    fa_copy = produce(0, 0, emit_fwd)
+    sibs_c = relay_second(2, first_c)
+    fb_copy = produce(0, 1, emit_fwd)
+    for c in sibs_b:
+        c.wait_recv()
+    others(lambda j: normalize(1, j))
+    for c in sibs_c:
+        c.wait_recv()
+    fa_sent = token_first(0, fa_copy)
+    fb_sent = expert_first(0, fb_copy)
+    for e in range(per):
+        others(functools.partial(bwd_part, e))
+
+    flipped = jnp.transpose(Sc[...].reshape(T, 128))[0:8]
     for p in range(2):
         for j in range(J):
             at = (p * J + j) * tok
@@ -426,36 +536,14 @@
                 )
     RS[me, x] = Sb[me]
 
-    def emit_bwd(at):
-        total = None
-        for e in range(per):
-            for grads, w in ((gg, wg), (gu, wu)):
-                piece = mm(grads[e], w[e, :, pl.ds(at, tile)])
-                total = piece if total is None else total + piece
-        return total
-
-    p_bwd = produce(1, emit_bwd)
-
-    next_rows = X[0, k, j0, :, cols(x)].astype(f32) + gathered(0, cross_fwd)
-    zbuf[0] = next_rows.astype(bf16)
-
-    def send_next():
-        return rcopy(
-            zbuf.at[0], out_next.at[0], sz.at[0], rz.at[0], {"segment": lax.rem(seg + 1, n_seg)}
-        )
-
-    def send_prev():
-        return rcopy(
-            zbuf.at[1],
-            out_prev.at[0],
-            sz.at[1],
-            rz.at[1],
-            {"segment": lax.rem(seg - 1 + n_seg, n_seg)},
-        )
-
-    @pl.when(seg < n_seg - 1)
-    def _():
-        send_next().start()
+    fa_sent = then_expert(0, fa_sent)
+    fb_sent = then_token(0, fb_sent)
+    ba_copy = produce(1, 0, emit_bwd)
+    finish_next(0, last_a(0, fa_sent))
+    finish_next(1, last_b(0, fb_sent))
+    bb_copy = produce(1, 1, emit_bwd)
+    ba_sent = token_first(1, ba_copy)
+    bb_sent = expert_first(1, bb_copy)
 
     @pl.when(seg == 0)
     def _():
@@ -464,8 +552,6 @@
     @pl.when(seg == n_seg - 1)
     def _():
         out_prev[...] = jnp.zeros(out_prev.shape, bf16)
-
-    sent_bwd = exchange(1, p_bwd)
 
     for c in cs:
         c.wait_recv()
@@ -496,25 +582,41 @@
     cot_own = X[2, k, j0, :, cols(x)].astype(f32)
     base = cot_own + inverse_b * (router_own * gain_own - scaled_own * mean_all)
 
-    cross_bwd = cross(1, sent_bwd)
-    zbuf[1] = (base + inverse_b * gain_own * gathered(1, cross_bwd)).astype(bf16)
+    scale_own = inverse_b * gain_own
+    own_base[...] = base
+    ba_sent = then_expert(1, ba_sent)
+    bb_sent = then_token(1, bb_sent)
+
+    def finish_prev(h, mixed):
+        at = slice(h * H, (h + 1) * H)
+        zbuf[1, :, at] = (own_base[:, at] + scale_own[:, at] * mixed).astype(bf16)
+
+        @pl.when(seg > 0)
+        def _():
+            send_prev(h).start()
+
+    finish_prev(0, last_a(1, ba_sent))
+    finish_prev(1, last_b(1, bb_sent))
+
+    for c in started:
+        c.wait_send()
+
+    @pl.when(seg < n_seg - 1)
+    def _():
+        for h in range(2):
+            send_next(h).wait_send()
+            send_prev(h).wait_recv()
 
     @pl.when(seg > 0)
     def _():
-        send_prev().start()
-
-    for c in started:
-        c.wait_send()
-
-    @pl.when(seg < n_seg - 1)
-    def _():
-        send_next().wait_send()
-        send_prev().wait_recv()
-
-    @pl.when(seg > 0)
-    def _():
-        send_prev().wait_send()
-        send_next().wait_recv()
+        for h in range(2):
+            send_prev(h).wait_send()
+            send_next(h).wait_recv()
+
+
+def settle(next_in, prev_in, next_out, prev_out):
+    next_out[...] = next_in[...]
+    prev_out[...] = prev_in[...]
 
 
 def body(
@@ -553,21 +655,28 @@
         V((per, F, D), bf16),
         V((per, F, D), bf16),
         V((per, F, D), bf16),
-        V((per, T, F), bf16),
-        V((per, T, F), bf16),
-        V((2, n_t, 2, J, tok, W), bf16),
-        V((2, n_t, J, tok, W), bf16),
-        V((2, toks, J, tok, W), bf16),
-        V((2, toks, J, tok, W), bf16),
-        V((2, J, tok, W), bf16),
-        V((2, peers, tok, W), bf16),
-        V((T, 128), f32),
+        V((per, 2, J, tok, F), bf16),
+        V((per, 2, J, tok, F), bf16),
+        V((per, 2, J, tok, F), bf16),
+        V((2, 2, 2, n_t, J, tok, W // 2), bf16),
+        V((2, 2, n_t, J, tok, W // 2), bf16),
+        V((2, toks, J, tok, W // 2), bf16),
+        V((2, toks, J, tok, W // 2), bf16),
+        V((2, J, tok, W // 2), bf16),
+        V((2, peers, tok, W // 2), bf16),
+        V((2, peers, n_t, tok, W // 2), bf16),
+        V((2, peers, n_t, tok, W // 2), bf16),
+        V((2, n_t, tok, W // 2), bf16),
+        V((2, toks, tok, W // 2), bf16),
+        V((2, J, tok, 128), f32),
         V((n_e, 8, tok), f32),
         V((n_e, n_t, 8, tok), f32),
         V((128, 128), f32),
         V((6, tok, 128), f32),
+        V((tok, W), f32),
         V((2, tok, W), bf16),
-        dma((3,)),
+        V((128, 128), f32),
+        dma((3, per)),
         dma((3,)),
         dma((3,)),
         dma((3,)),
@@ -579,29 +688,33 @@
         dma((3, peers, n_t)),
         dma((3, peers, toks)),
         dma((3, peers, toks)),
-        dma((2, n_t)),
-        dma((2, n_t)),
+        dma((2, 2)),
+        dma((2, 2)),
         dma((2, toks)),
         dma((2, toks)),
         dma((2, peers)),
         dma((2, peers)),
+        dma((2, peers)),
+        dma((2, peers)),
+        dma((2, toks)),
+        dma((2, toks)),
         dma((n_e, n_t)),
         dma((n_e, n_t)),
-        dma((2,)),
-        dma((2,)),
+        dma((2, 2)),
+        dma((2, 2)),
     ]
     codes = jnp.concatenate(
         [
-            ids[0] + jnp.where(slots[0] < cap, 0, E)
+            (ids[0] + jnp.where(slots[0] < cap, 0, E)).T
             for ids, slots in ((fwd_ids, fwd_slots), (bwd_ids, bwd_slots))
         ],
-        axis=1,
+        axis=0,
     )
     vm = pl.BlockSpec(memory_space=pltpu.VMEM)
     hbm = pl.BlockSpec(memory_space=pl.ANY)
     out = jax.ShapeDtypeStruct((1, tok, W), bf16)
     sizes = (n_seg, n_e, n_t, per, E, tok, D, F, K)
-    return pl.pallas_call(
+    moved = pl.pallas_call(
         functools.partial(kernel, sizes),
         out_shape=(out, out),
         in_specs=[hbm] * 3 + [vm] * 3 + [hbm] * 3,
@@ -622,6 +735,9 @@
         jnp.swapaxes(w_up, 1, 2),
         w_down,
     )
+    return pl.pallas_call(
+        settle, out_shape=(out, out), in_specs=[vm] * 2, out_specs=(vm, vm), name="settle"
+    )(*moved)
 
 
 def solution(mesh):

time: 61.1 us -> 67.5 us (1.10)
  Pallas kernels: 55.7 us -> 65.3 us
  local copies, waits for them, and re-layouts: 3.85 us -> 0 us
    pallas_call x1, Pallas kernels: 55.7 us -> 63.6 us  [body(): pl.pallas_call(functools.partial(kernel, sizes), out_shape=(out, out), in...]
    unnamed x2 -> x0, local copies, waits for them, and re-layouts: 3.14 us -> none
    pallas_call x0 -> x1, Pallas kernels: none -> 1.68 us  [body(): pl.pallas_call(settle, out_shape=(out, out), in_specs=[vm] * 2, out_specs...]
    transpose x0 -> x1, other arithmetic: none -> 0.74 us  [body(): codes = jnp.concatenate([(ids[0] + jnp.where(slots[0] < cap, 0, E)).T for...]
    add x1 -> x0, other arithmetic: 0.74 us -> none  [body(): ids[0] + jnp.where(slots[0] < cap, 0, E)]
    concatenate x1 -> x0, local copies, waits for them, and re-layouts: 0.71 us -> none  [body(): jnp.concatenate([ids[0] + jnp.where(slots[0] < cap, 0, E) for ids, slots...]
where the time goes in v2:
time: 67.5 us; the launch traced here: 67.3 us
  Pallas kernels  65.3 us (97%)
  other arithmetic  1.35 us (2%)
    pallas_call x1, Pallas kernels, body(): pl.pallas_call(functools.partial(kernel, sizes), out_shape=(out, out), in...  63.6 us
    pallas_call x1, Pallas kernels, body(): pl.pallas_call(settle, out_shape=(out, out), in_specs=[vm] * 2, out_specs...  1.68 us

profile of v2, /device:TPU:0, one launch (start us, length us, event | category | flops | bytes accessed | tf_op | source)
XLA Modules:
  0.0 67.3 jit_solution(5667956160500586816)
XLA Ops:
  0.6 0.7 %fusion = (s32[6,64]{1,0:T(8,128)S(1)}, s32[6,64]{1,0:T(8,128)S(1)}) fusion(s32[1,64,6]{1,0,2:T(1,128)} %param.16, s32[1,64,6]{1,0,2:T(1,128)} %param.17, s32[1,64,6]{1,0,2:T(1,128)} %param.14, s32[1,64,6]{1,0,2:T(1,128)} %param.13), kind=kLoop, calls=%fused_computation.2 | loop fusion | flops 2304 | bytes 9216 | tf_op jit(solution)/shard_map/transpose | solution.py:708
  1.4 0.6 pad_add_fusion.codes
  2.0 63.6 %relay_moe.1 = (bf16[1,64,1024]{2,1,0:T(8,128)(2,1)}, bf16[1,64,1024]{2,1,0:T(8,128)(2,1)}) custom-call(bf16[1,64,2048]{2,1,0:T(8,128)(2,1)} %fa.1, bf16[1,64,2048]{2,1,0:T(8,128)(2,1)} %ba.1, bf16[1,64,2048]{2,1,0:T(8,128)(2,1)} %bg.1, s32[12,64]{1,0:T(8,128)} %pad_add_fusion.codes, f32[1,2048]{1,0:T(1,128)} %gain.1, f32[8,2048]{1,0:T(8,128)} %bitcast.15, ...), custom_call_target="tpu_custom_call" | custom-call | tf_op jit(solution)/shard_map/relay_moe/pallas_call | solution.py:717
  65.6 1.7 %settle.1 = (bf16[1,64,1024]{2,1,0:T(8,128)(2,1)}, bf16[1,64,1024]{2,1,0:T(8,128)(2,1)}) custom-call(bf16[1,64,1024]{2,1,0:T(8,128)(2,1)} %get-tuple-element.4.next_in, bf16[1,64,1024]{2,1,0:T(8,128)(2,1)} %get-tuple-element.5.prev_in), custom_call_target="tpu_custom_call" | custom-call | tf_op jit(solution)/shard_map/settle/pallas_call | solution.py:738

commit v3 on v2

--- a/solution.py
+++ b/solution.py
@@ -273,40 +273,39 @@
         for p in range(2):
             N[p, j] = normed_block(s, X[s, p, j])[0]
 
-    M = 2 * tok
+    M = T
     wide_lane = lax.broadcasted_iota(jnp.int32, (M, 128), 1)
 
-    def column(s, e, j):
+    def column(s, e):
         want = s * E + me * per + e
-        picked = jnp.where(wide_lane == want, G[:, j].reshape(M, 128), 0.0)
+        picked = jnp.where(wide_lane == want, G[...].reshape(M, 128), 0.0)
         return jnp.sum(picked, axis=1, keepdims=True)
 
-    def put(ref, e, j, value):
-        ref[e, :, j] = value.astype(bf16).reshape(2, tok, F)
-
-    def fwd_part(e, j):
-        rows = N[:, j].reshape(M, D)
+    def put(ref, e, value):
+        ref[e] = value.astype(bf16)
+
+    def fwd_part(e):
+        rows = N[...].reshape(M, D)
         gate = mm(rows, wg[e], NT)
         up = mm(rows, wu[e], NT)
-        put(act, e, j, gate * jax.nn.sigmoid(gate) * up * column(0, e, j))
-
-    def bwd_part(e, j):
-        rows = N[:, j].reshape(M, D)
+        put(act, e, gate * jax.nn.sigmoid(gate) * up * column(0, e))
+
+    def bwd_part(e):
+        rows = N[...].reshape(M, D)
         gate = mm(rows, wg[e], NT)
         up = mm(rows, wu[e], NT)
-        grad_act = mm(X[2, :, j].reshape(M, D), wd[e], NT)
+        grad_act = mm(X[2].reshape(M, D), wd[e], NT)
         sigma = jax.nn.sigmoid(gate)
         silu = gate * sigma
         ggv = grad_act * up * sigma * (1.0 + gate * (1.0 - sigma))
         guv = grad_act * silu
-        col = column(1, e, j)
+        col = column(1, e)
         dg = jnp.sum(guv * up, axis=1, keepdims=True)
         corr = col * jnp.sum(ggv * gate + guv * up, axis=1, keepdims=True)
         both = jnp.where(wide_lane == e, dg, 0.0) + jnp.where(wide_lane == per, corr, 0.0)
-        both = both.reshape(2, tok, 128)
-        Sc[:, j] = both if e == 0 else Sc[:, j] + both
-        put(gg, e, j, ggv * col)
-        put(gu, e, j, guv * col)
+        Sc[...] = both if e == 0 else Sc[...] + both
+        put(gg, e, ggv * col)
+        put(gu, e, guv * col)
 
     def others(fn):
         if J == 2:
@@ -453,7 +452,7 @@
     def emit_fwd(at):
         total = None
         for e in range(per):
-            piece = mm(act[e].reshape(T, F), wd[e, :, pl.ds(at, H)])
+            piece = mm(act[e], wd[e, :, pl.ds(at, H)])
             total = piece if total is None else total + piece
         return total
 
@@ -461,7 +460,7 @@
         total = None
         for e in range(per):
             for grads, w in ((gg, wg), (gu, wu)):
-                piece = mm(grads[e].reshape(T, F), w[e, :, pl.ds(at, H)])
+                piece = mm(grads[e], w[e, :, pl.ds(at, H)])
                 total = piece if total is None else total + piece
         return total
 
@@ -475,45 +474,39 @@
 
     c0[0].wait_recv()
     normalize(0, j0)
+    first_a = relay_first(0)
     for c in cg:
         c.wait_recv()
+    first_b = relay_first(1)
+    for c in relay_second(0, first_a):
+        c.wait_recv()
+    others(lambda j: normalize(0, j))
     for e in range(per):
         weights[0][e].wait()
         weights[1][e].wait()
-        fwd_part(e, j0)
+        fwd_part(e)
         if e == 0:
-            first_a = relay_first(0)
+            first_c = relay_first(2)
+            sibs_b = relay_second(1, first_b)
     c0[1].wait_recv()
     c0[2].wait_recv()
-    normalize(1, j0)
     for e in range(per):
         weights[2][e].wait()
-        bwd_part(e, j0)
-        if e == 0:
-            first_b = relay_first(1)
-    sibs_a = relay_second(0, first_a)
-    for c in sibs_a:
-        c.wait_recv()
-    others(lambda j: normalize(0, j))
-    others(lambda j: fwd_part(0, j))
-    first_c = relay_first(2)
-    sibs_b = relay_second(1, first_b)
-    for e in range(1, per):
-        others(functools.partial(fwd_part, e))
     fa_copy = produce(0, 0, emit_fwd)
     sibs_c = relay_second(2, first_c)
     fb_copy = produce(0, 1, emit_fwd)
     for c in sibs_b:
         c.wait_recv()
+    normalize(1, j0)
     others(lambda j: normalize(1, j))
     for c in sibs_c:
         c.wait_recv()
     fa_sent = token_first(0, fa_copy)
     fb_sent = expert_first(0, fb_copy)
     for e in range(per):
-        others(functools.partial(bwd_part, e))
-
-    flipped = jnp.transpose(Sc[...].reshape(T, 128))[0:8]
+        bwd_part(e)
+
+    flipped = jnp.transpose(Sc[...])[0:8]
     for p in range(2):
         for j in range(J):
             at = (p * J + j) * tok
@@ -655,9 +648,9 @@
         V((per, F, D), bf16),
         V((per, F, D), bf16),
         V((per, F, D), bf16),
-        V((per, 2, J, tok, F), bf16),
-        V((per, 2, J, tok, F), bf16),
-        V((per, 2, J, tok, F), bf16),
+        V((per, T, F), bf16),
+        V((per, T, F), bf16),
+        V((per, T, F), bf16),
         V((2, 2, 2, n_t, J, tok, W // 2), bf16),
         V((2, 2, n_t, J, tok, W // 2), bf16),
         V((2, toks, J, tok, W // 2), bf16),
@@ -668,7 +661,7 @@
         V((2, peers, n_t, tok, W // 2), bf16),
         V((2, n_t, tok, W // 2), bf16),
         V((2, toks, tok, W // 2), bf16),
-        V((2, J, tok, 128), f32),
+        V((T, 128), f32),
         V((n_e, 8, tok), f32),
         V((n_e, n_t, 8, tok), f32),
         V((128, 128), f32),

time: 67.5 us -> 57.2 us (0.85)
  Pallas kernels: 65.3 us -> 55 us
    pallas_call x1, Pallas kernels: 63.6 us -> 53.3 us  [body(): pl.pallas_call(functools.partial(kernel, sizes), out_shape=(out, out), in...]
where the time goes in v3:
time: 57.2 us; the launch traced here: 57 us
  Pallas kernels  55 us (96%)
  other arithmetic  1.35 us (2%)
  between operations  0.64 us (1%)
    pallas_call x1, Pallas kernels, body(): pl.pallas_call(functools.partial(kernel, sizes), out_shape=(out, out), in...  53.3 us
    pallas_call x1, Pallas kernels, body(): pl.pallas_call(settle, out_shape=(out, out), in_specs=[vm] * 2, out_specs...  1.68 us

profile of v3, /device:TPU:0, one launch (start us, length us, event | category | flops | bytes accessed | tf_op | source)
XLA Modules:
  0.0 57.0 jit_solution(10952177040552715491)
XLA Ops:
  0.6 0.7 %fusion = (s32[6,64]{1,0:T(8,128)S(1)}, s32[6,64]{1,0:T(8,128)S(1)}) fusion(s32[1,64,6]{1,0,2:T(1,128)} %param.16, s32[1,64,6]{1,0,2:T(1,128)} %param.17, s32[1,64,6]{1,0,2:T(1,128)} %param.14, s32[1,64,6]{1,0,2:T(1,128)} %param.13), kind=kLoop, calls=%fused_computation.2 | loop fusion | flops 2304 | bytes 9216 | tf_op jit(solution)/shard_map/transpose | solution.py:701
  1.4 0.6 %pad_add_fusion.codes = s32[12,64]{1,0:T(8,128)} fusion(s32[6,64]{1,0:T(8,128)S(1)} %get-tuple-element.6, s32[6,64]{1,0:T(8,128)S(1)} %get-tuple-element.7), kind=kLoop, calls=%fused_computation | loop fusion | flops 768 | bytes 6144 | tf_op jit(solution)/shard_map/concatenate | solution.py:699
  2.0 53.3 %relay_moe.1 = (bf16[1,64,1024]{2,1,0:T(8,128)(2,1)}, bf16[1,64,1024]{2,1,0:T(8,128)(2,1)}) custom-call(bf16[1,64,2048]{2,1,0:T(8,128)(2,1)} %fa.1, bf16[1,64,2048]{2,1,0:T(8,128)(2,1)} %ba.1, bf16[1,64,2048]{2,1,0:T(8,128)(2,1)} %bg.1, s32[12,64]{1,0:T(8,128)} %pad_add_fusion.codes, f32[1,2048]{1,0:T(1,128)} %gain.1, f32[8,2048]{1,0:T(8,128)} %bitcast.15, ...), custom_call_target="tpu_custom_call" | custom-call | tf_op jit(solution)/shard_map/relay_moe/pallas_call | solution.py:710
  55.3 1.7 %settle.1 = (bf16[1,64,1024]{2,1,0:T(8,128)(2,1)}, bf16[1,64,1024]{2,1,0:T(8,128)(2,1)}) custom-call(bf16[1,64,1024]{2,1,0:T(8,128)(2,1)} %get-tuple-element.4.next_in, bf16[1,64,1024]{2,1,0:T(8,128)(2,1)} %get-tuple-element.5.prev_in), custom_call_target="tpu_custom_call" | custom-call | tf_op jit(solution)/shard_map/settle/pallas_call | solution.py:731
